TPU v7x, 32 devices: a whole 2x2x4 slice. The times are simulated.
32 devices in a mesh: lat: 4 (over y, core), lon: 8 (over z, x).
Axes of the slice: x: 2, y: 2, z: 4, core: 2. Of those that a mesh axis runs over, the one named last changes fastest.
Arguments:
- background: bfloat16 [256, 512, 128], P('lat', 'lon'), may hold values from -6 to 6
- diffusivity: float32 [256, 512, 128], P('lat', 'lon'), may hold values from 0.12 to 0.245
- tile_index: int32 [16384, 1], P(('lat', 'lon')), may hold values from 0 to 31; in each aligned block of 512 rows (0 to 511, 512 to 1023, ...) at most 32 rows name the same one
- anchor: int32 [16384], P(('lat', 'lon')), may hold values from 0 to 3968
- weights: float32 [16384, 4], P(('lat', 'lon')), may hold values from 0.2 to 1
- observed: float32 [16384, 128], P(('lat', 'lon')), may hold values from -6 to 6
- accept: int32 [16384, 128], P(('lat', 'lon')), may hold values 0 or 1
- absorb: float32 [128, 128], replicated, may hold values from 0.001 to 0.1
- sensitivity: float32 [128], replicated, may hold values from -0.5 to 0.5
- inverse_variance: float32 [128], replicated, may hold values from 0.25 to 4
Outputs:
- departure: float32 [16384, 128], P(('lat', 'lon'))
- increment: float32 [256, 512, 128], P('lat', 'lon')
Inputs may be any that keep to these rules, and one draw needn't show every extreme that they name: `tile_index`: among the 512 footprints of one device no tile is named more than 32 times, a bound that some block reaches.
All inputs are finite; a program needn't handle non-finite values. No bound on the sum of `accept` on one device may be relied on, other than what follows from the above.
Results may differ from a plain program's by a relative error of at most 0.0003.
Values may be sent and summed in bfloat16 or wider, within the bound.
No kernel may reach another device: no remote copies, remote signals or barrier semaphores. Data moves between devices by JAX's collectives and lax.ppermute only.
A program may use at most 64 MiB of HBM per device.

v0:
```python
import jax
import jax.numpy as jnp
from jax import lax
from jax.sharding import PartitionSpec as P

STEPS = 8


NEIGHBOURS = ((-1, 0), (1, 0), (0, -1), (0, 1))


def padded_2(block, sides, width, periodic):
    for axis, dim in sides:
        count = lax.axis_size(axis)
        forward = [(i, i + 1) for i in range(count - 1)]
        if periodic:
            forward.append((count - 1, 0))
        backward = [(target, source) for source, target in forward]
        low = lax.ppermute(
            lax.slice_in_dim(block, block.shape[dim] - width, None, axis=dim), axis, forward
        )
        high = lax.ppermute(lax.slice_in_dim(block, 0, width, axis=dim), axis, backward)
        block = jnp.concatenate([low, block, high], axis=dim)
    return block


def evolve(profile, absorb, sensitivity):
    layer_depth = absorb[None, :, :] * jnp.exp(sensitivity[None, None, :] * profile[:, :, None])
    optical = jnp.cumsum(layer_depth, axis=1)
    transmit = jnp.exp(-optical)
    transmit_above = jnp.concatenate(
        [jnp.ones_like(transmit[:, :1, :]), transmit[:, :-1, :]], axis=1
    )
    layered = jnp.sum(profile[:, :, None] * (transmit_above - transmit), axis=1)
    return layered + profile[:, -1:] * transmit[:, -1, :]


def assess(profile, observed, accept, absorb, sensitivity, inverse_variance):
    evolved, pullback = jax.vjp(lambda prof_in: evolve(prof_in, absorb, sensitivity), profile)
    departure = observed - evolved
    (adjoint,) = pullback(-(accept.astype(jnp.float32) * inverse_variance[None, :] * departure))
    return (departure, adjoint)


def extend(grid_field, halo_width):
    padded = padded_2(grid_field, (("lat", 0),), halo_width, False)
    return padded_2(padded, (("lon", 1),), halo_width, True)


def relax(grid_field, diffusivity):
    height = grid_field.shape[0]
    breadth = grid_field.shape[1]
    centre = grid_field[1:-1, 1:-1]
    kappa_centre = diffusivity[1:-1, 1:-1]
    summed = centre
    for d_row, d_col in NEIGHBOURS:
        neighbour = grid_field[1 + d_row : height - 1 + d_row, 1 + d_col : breadth - 1 + d_col]
        kappa_near = diffusivity[1 + d_row : height - 1 + d_row, 1 + d_col : breadth - 1 + d_col]
        summed = summed + 0.5 * (kappa_centre + kappa_near) * (neighbour - centre)
    return summed


def local(
    background,
    diffusivity,
    tile_index,
    anchor,
    weights,
    observed,
    accept,
    absorb,
    sensitivity,
    inverse_variance,
):
    lat_count = lax.axis_size("lat")
    lon_count = lax.axis_size("lon")
    dev_count = lat_count * lon_count
    foot_count = tile_index.shape[0]
    capacity = max(2, 2 * foot_count // dev_count)
    tile_rows, tile_cols, levels = background.shape
    owner_tile = tile_index[:, 0]
    onehot = (owner_tile[:, None] == jnp.arange(dev_count, dtype=jnp.int32)[None, :]).astype(
        jnp.int32
    )
    slot_rank = jnp.sum((jnp.cumsum(onehot, axis=0) - onehot) * onehot, axis=1)
    slot_index = owner_tile * capacity + slot_rank
    base_cell = anchor // (tile_cols - 1) * tile_cols + anchor % (tile_cols - 1)
    local_ids = jnp.stack(
        [base_cell, base_cell + 1, base_cell + tile_cols, base_cell + tile_cols + 1], axis=1
    )
    shares = weights / jnp.sum(weights, axis=1, keepdims=True)
    request = (
        jnp.zeros((dev_count * capacity, 4), jnp.int32)
        .at[slot_index]
        .set(local_ids)
        .reshape(dev_count, capacity, 4)
    )
    asked_ids = lax.all_to_all(
        request, ("lat", "lon"), split_axis=0, concat_axis=0, tiled=True
    ).reshape(-1)
    flat_bg = background.reshape(tile_rows * tile_cols, levels)
    columns = jnp.take(flat_bg, asked_ids, axis=0).reshape(dev_count, capacity, 4, levels)
    share_slots = (
        jnp.zeros((dev_count * capacity, 4), jnp.float32)
        .at[slot_index]
        .set(shares)
        .reshape(dev_count, capacity, 4)
    )
    asked_shares = lax.all_to_all(
        share_slots, ("lat", "lon"), split_axis=0, concat_axis=0, tiled=True
    )
    local_profiles = jnp.sum(asked_shares[:, :, :, None] * columns.astype(jnp.float32), axis=2)
    returned = lax.all_to_all(
        local_profiles, ("lat", "lon"), split_axis=0, concat_axis=0, tiled=True
    )
    profile = returned.reshape(dev_count * capacity, levels)[slot_index]
    block_count = foot_count // 64
    channels = observed.shape[1]
    departure, adjoint = lax.map(
        lambda packed: assess(
            packed[0], packed[1], packed[2], absorb, sensitivity, inverse_variance
        ),
        (
            profile.reshape(block_count, 64, levels),
            observed.reshape(block_count, 64, channels),
            accept.reshape(block_count, 64, channels),
        ),
    )
    departure = departure.reshape(foot_count, channels)
    adjoint = adjoint.reshape(foot_count, levels)
    grad_slots = (
        jnp.zeros((dev_count * capacity, levels), jnp.float32)
        .at[slot_index]
        .set(adjoint)
        .reshape(dev_count, capacity, levels)
    )
    arrived = lax.all_to_all(grad_slots, ("lat", "lon"), split_axis=0, concat_axis=0, tiled=True)
    adjoint_terms = asked_shares[:, :, :, None] * arrived[:, :, None, :]
    increment = (
        jnp.zeros((tile_rows * tile_cols, levels), jnp.float32)
        .at[asked_ids]
        .add(-adjoint_terms.reshape(-1, levels))
    )
    grid_field = increment.reshape(tile_rows, tile_cols, levels)
    kappa_ext = extend(diffusivity, 1)
    for repeat_index in range(STEPS):
        grid_field = relax(extend(grid_field, 1), kappa_ext)
    return (departure, grid_field)


def solution(mesh):
    in_specs = (
        P("lat", "lon", None),
        P("lat", "lon", None),
        P(("lat", "lon"), None),
        P(("lat", "lon")),
        P(("lat", "lon"), None),
        P(("lat", "lon"), None),
        P(("lat", "lon"), None),
        P(),
        P(),
        P(),
    )
    out_specs = (P(("lat", "lon"), None), P("lat", "lon", None))
    return jax.shard_map(local, mesh=mesh, in_specs=in_specs, out_specs=out_specs, check_vma=False)
```

profile of v0, /device:TPU:1, one launch (start us, length us, event | category | flops | bytes accessed | tf_op | source)
XLA Modules:
  0.0 528.2 jit_solution(6792588688188333729)
XLA Ops:
  8.0 7.1 %all-to-all-start.1 = ((s32[32,1,128]{2,1,0:T(1,128)}), s32[32,1,128]{2,1,0:T(1,128)S(1)}, u32[]{:S(2)}, u32[]{:S(2)}) async-start(s32[32,1,128]{2,1,0:T(1,128)} %reshape.279), calls=%async_computation.1 | async-start | bytes 32768 | tf_op jit(solution)/shard_map/all_to_all | solution.py:98
  21.8 3.6 all-to-all-start
  27.1 5.0 all-to-all-done
  34.3 12.1 %gather_fusion = bf16[4096,128]{1,0:T(8,128)(2,1)S(1)} fusion(bf16[4096,128]{1,0:T(8,128)(2,1)S(1)} %bitcast.125, s32[4096]{0:T(1024)S(1)} %broadcast_clamp_fusion), kind=kCustom, calls=%fused_computation | custom fusion | bytes 2113536 | tf_op jit(solution)/shard_map/jit(_take)/gather | solution.py:102
  46.4 3.6 multiply_reduce_fusion.3
  53.1 15.8 %all-to-all-done.2 = f32[32,32,128]{2,1,0:T(8,128)S(1)} async-done(((f32[32,32,128]{2,1,0:T(8,128)}), f32[32,32,128]{2,1,0:T(8,128)S(1)}, u32[]{:S(2)}, u32[]{:S(2)}) %all-to-all-start.2) | async-done | bytes 524320 | tf_op jit(solution)/shard_map/all_to_all | solution.py:113
  70.6 255.8 %while.12 = (s32[]{:T(128)}, f32[8,64,128]{2,1,0:T(8,128)}, f32[8,64,128]{2,1,0:T(8,128)}, f32[8,64,128]{2,1,0:T(8,128)}, f32[8,64,128]{2,1,0:T(8,128)}, /*index...) while((s32[]{:T(128)}, f32[8,64,128]{2,1,0:T(8,128)}, ...), condition=%wide.region_14.15_spmd, body=%wide.region_7.14_spmd.sunk | while | flops 288513984 | bytes 68161432 | solution.py:119
  95.3 19.7 %multiply_reduce_fusion.9 = f32[64,128]{0,1:T(8,128)S(1)} fusion(f32[128]{0:T(128)S(1)} %get-tuple-element.248, f32[128,128]{1,0:T(8,128)S(1)} %get-tuple-element.247, f32[64,128]{0,1:T(8,128)S(1)} %bitcast.130, f32[64,128,128]{2,0,1:T(8,128)S(1)} %negate_exponential_fusion.2, f32[64,127,128]{2,0,1:T(8,128)S(1)} %split.5, ...), kind=kOutput, calls=%fused_computation.6.clone.1 | output fusion | flops 144695296 | bytes 8552960 | tf_op jit(solution)/shard_map/while/body/eval_jaxpr/transpose(jvp(jit(cumsum)))/reduce_window_sum | solution.py:29
  125.3 19.7 %multiply_reduce_fusion.9 = f32[64,128]{0,1:T(8,128)S(1)} fusion(f32[128]{0:T(128)S(1)} %get-tuple-element.248, f32[128,128]{1,0:T(8,128)S(1)} %get-tuple-element.247, f32[64,128]{0,1:T(8,128)S(1)} %bitcast.130, f32[64,128,128]{2,0,1:T(8,128)S(1)} %negate_exponential_fusion.2, f32[64,127,128]{2,0,1:T(8,128)S(1)} %split.5, ...), kind=kOutput, calls=%fused_computation.6.clone.1 | output fusion | flops 144695296 | bytes 8552960 | tf_op jit(solution)/shard_map/while/body/eval_jaxpr/transpose(jvp(jit(cumsum)))/reduce_window_sum | solution.py:29
  155.3 19.7 %multiply_reduce_fusion.9 = f32[64,128]{0,1:T(8,128)S(1)} fusion(f32[128]{0:T(128)S(1)} %get-tuple-element.248, f32[128,128]{1,0:T(8,128)S(1)} %get-tuple-element.247, f32[64,128]{0,1:T(8,128)S(1)} %bitcast.130, f32[64,128,128]{2,0,1:T(8,128)S(1)} %negate_exponential_fusion.2, f32[64,127,128]{2,0,1:T(8,128)S(1)} %split.5, ...), kind=kOutput, calls=%fused_computation.6.clone.1 | output fusion | flops 144695296 | bytes 8552960 | tf_op jit(solution)/shard_map/while/body/eval_jaxpr/transpose(jvp(jit(cumsum)))/reduce_window_sum | solution.py:29
  185.2 19.7 %multiply_reduce_fusion.9 = f32[64,128]{0,1:T(8,128)S(1)} fusion(f32[128]{0:T(128)S(1)} %get-tuple-element.248, f32[128,128]{1,0:T(8,128)S(1)} %get-tuple-element.247, f32[64,128]{0,1:T(8,128)S(1)} %bitcast.130, f32[64,128,128]{2,0,1:T(8,128)S(1)} %negate_exponential_fusion.2, f32[64,127,128]{2,0,1:T(8,128)S(1)} %split.5, ...), kind=kOutput, calls=%fused_computation.6.clone.1 | output fusion | flops 144695296 | bytes 8552960 | tf_op jit(solution)/shard_map/while/body/eval_jaxpr/transpose(jvp(jit(cumsum)))/reduce_window_sum | solution.py:29
  215.2 19.7 %multiply_reduce_fusion.9 = f32[64,128]{0,1:T(8,128)S(1)} fusion(f32[128]{0:T(128)S(1)} %get-tuple-element.248, f32[128,128]{1,0:T(8,128)S(1)} %get-tuple-element.247, f32[64,128]{0,1:T(8,128)S(1)} %bitcast.130, f32[64,128,128]{2,0,1:T(8,128)S(1)} %negate_exponential_fusion.2, f32[64,127,128]{2,0,1:T(8,128)S(1)} %split.5, ...), kind=kOutput, calls=%fused_computation.6.clone.1 | output fusion | flops 144695296 | bytes 8552960 | tf_op jit(solution)/shard_map/while/body/eval_jaxpr/transpose(jvp(jit(cumsum)))/reduce_window_sum | solution.py:29
  245.2 19.7 %multiply_reduce_fusion.9 = f32[64,128]{0,1:T(8,128)S(1)} fusion(f32[128]{0:T(128)S(1)} %get-tuple-element.248, f32[128,128]{1,0:T(8,128)S(1)} %get-tuple-element.247, f32[64,128]{0,1:T(8,128)S(1)} %bitcast.130, f32[64,128,128]{2,0,1:T(8,128)S(1)} %negate_exponential_fusion.2, f32[64,127,128]{2,0,1:T(8,128)S(1)} %split.5, ...), kind=kOutput, calls=%fused_computation.6.clone.1 | output fusion | flops 144695296 | bytes 8552960 | tf_op jit(solution)/shard_map/while/body/eval_jaxpr/transpose(jvp(jit(cumsum)))/reduce_window_sum | solution.py:29
  275.1 19.7 %multiply_reduce_fusion.9 = f32[64,128]{0,1:T(8,128)S(1)} fusion(f32[128]{0:T(128)S(1)} %get-tuple-element.248, f32[128,128]{1,0:T(8,128)S(1)} %get-tuple-element.247, f32[64,128]{0,1:T(8,128)S(1)} %bitcast.130, f32[64,128,128]{2,0,1:T(8,128)S(1)} %negate_exponential_fusion.2, f32[64,127,128]{2,0,1:T(8,128)S(1)} %split.5, ...), kind=kOutput, calls=%fused_computation.6.clone.1 | output fusion | flops 144695296 | bytes 8552960 | tf_op jit(solution)/shard_map/while/body/eval_jaxpr/transpose(jvp(jit(cumsum)))/reduce_window_sum | solution.py:29
  305.1 19.7 %multiply_reduce_fusion.9 = f32[64,128]{0,1:T(8,128)S(1)} fusion(f32[128]{0:T(128)S(1)} %get-tuple-element.248, f32[128,128]{1,0:T(8,128)S(1)} %get-tuple-element.247, f32[64,128]{0,1:T(8,128)S(1)} %bitcast.130, f32[64,128,128]{2,0,1:T(8,128)S(1)} %negate_exponential_fusion.2, f32[64,127,128]{2,0,1:T(8,128)S(1)} %split.5, ...), kind=kOutput, calls=%fused_computation.6.clone.1 | output fusion | flops 144695296 | bytes 8552960 | tf_op jit(solution)/shard_map/while/body/eval_jaxpr/transpose(jvp(jit(cumsum)))/reduce_window_sum | solution.py:29
  329.4 3.6 all-to-all-start.3
  333.8 3.6 collective-permute-start
  343.9 5.0 all-to-all-done.3
  351.7 29.5 %scatter_custom_fusion.3 = f32[4096,128]{1,0:T(8,128)} fusion(s32[4096]{0:T(1024)S(1)} %bitcast.144, f32[4096,128]{1,0:T(8,128)} %bitcast.134, f32[4096]{0:T(1024)S(1)} %mul.298, f32[]{:T(128)} %constant.51.clone.1), kind=kCustom, calls=%fused_computation.221 | custom fusion | flops 1572864 | bytes 4210692 | tf_op jit(solution)/shard_map/scatter-add | solution.py:142
  396.3 6.0 %fusion.114 = (f32[64,64,128]{2,1,0:T(8,128)S(1)}, f32[64,64,128]{2,1,0:T(8,128)S(1)}, f32[64,64,128]{2,1,0:T(8,128)S(1)}) fusion(f32[64,64,128]{2,1,0:T(8,128)S(1)} %bitcast.132, f32[66,1,128]{2,1,0:T(1,128)S(1)} %collective-permute-done.7, f32[1,64,128]{2,1,0:T(8,128)S(1)} %collective-permute-done.3, f32[1,64,128]{2,1,0:T(8,128)S(1)} %collective-permute-done.1, ...), kind=kLoop, calls=%fused_computation.192 | loop fusion | flops 16777216 | bytes 12914688 | tf_op jit(solution)/shard_map/add | solution.py:59
  402.4 4.5 collective-permute-start.8
  417.7 3.5 fusion.102
  429.7 4.5 collective-permute-start.15
  435.4 3.5 fusion.90
  447.1 4.6 collective-permute-start.19
  464.6 4.6 collective-permute-start.23
  470.4 3.8 fusion.66
  482.3 4.6 collective-permute-start.27
  499.8 4.6 collective-permute-start.31
  505.6 3.5 fusion.42
  517.3 4.6 collective-permute-start.35
  523.1 4.9 fusion.30
  (263 shorter events, 206.6 us)
Async XLA Ops:
  8.0 13.7 %all-to-all-start.1 = ((s32[32,1,128]{2,1,0:T(1,128)}), s32[32,1,128]{2,1,0:T(1,128)S(1)}, u32[]{:S(2)}, u32[]{:S(2)}) async-start(s32[32,1,128]{2,1,0:T(1,128)} %reshape.279), calls=%async_computation.1 | async-start | bytes 32768 | tf_op jit(solution)/shard_map/all_to_all | solution.py:98
  21.8 10.3 %all-to-all-start = ((f32[32,1,128]{2,1,0:T(1,128)}), f32[32,1,128]{2,1,0:T(1,128)S(1)}, u32[]{:S(2)}, u32[]{:S(2)}) async-start(f32[32,1,128]{2,1,0:T(1,128)} %reshape.281), calls=%async_computation | async-start | bytes 32768 | tf_op jit(solution)/shard_map/all_to_all | solution.py:109
  50.1 18.9 %all-to-all-start.2 = ((f32[32,32,128]{2,1,0:T(8,128)}), f32[32,32,128]{2,1,0:T(8,128)S(1)}, u32[]{:S(2)}, u32[]{:S(2)}) async-start(f32[32,32,128]{2,1,0:T(8,128)} %multiply_reduce_fusion.3), calls=%async_computation.2 | async-start | bytes 1048576 | tf_op jit(solution)/shard_map/all_to_all | solution.py:113
  329.4 19.6 %all-to-all-start.3 = ((f32[32,32,128]{2,1,0:T(8,128)}), f32[32,32,128]{2,1,0:T(8,128)}, u32[]{:S(2)}, u32[]{:S(2)}) async-start(f32[32,32,128]{2,1,0:T(8,128)} %bitcast.138), calls=%async_computation.3 | async-start | bytes 1048576 | tf_op jit(solution)/shard_map/all_to_all | solution.py:137
  333.8 6.8 %collective-permute-start = (f32[1,64,128]{2,1,0:T(8,128)S(1)}, f32[1,64,128]{2,1,0:T(8,128)S(1)}, u32[]{:S(2)}, u32[]{:S(2)}) collective-permute-start(f32[1,64,128]{2,1,0:T(8,128)S(1)} %get-tuple-element.150), channel_id=1, source_target_pairs={{0,8},{8,16},{16,24},{1,9},{9,17},{17,25},{2,10},{10,18},{18,26},{... | collective-permute-start | bytes 98312 | tf_op jit(solution)/shard_map/ppermute | solution.py:19
  337.4 5.9 %collective-permute-start.2 = (f32[1,64,128]{2,1,0:T(8,128)S(1)}, f32[1,64,128]{2,1,0:T(8,128)S(1)}, u32[]{:S(2)}, u32[]{:S(2)}) collective-permute-start(f32[1,64,128]{2,1,0:T(8,128)S(1)} %get-tuple-element.149), channel_id=1, source_target_pairs={{8,0},{16,8},{24,16},{9,1},{17,9},{25,17},{10,2},{18,10},{26,18},{... | collective-permute-start | bytes 98312 | tf_op jit(solution)/shard_map/ppermute | solution.py:22
  382.1 6.9 %collective-permute-start.1 = (f32[1,64,128]{2,1,0:T(8,128)S(1)}, f32[1,64,128]{2,1,0:T(8,128)S(1)}, u32[]{:S(2)}, u32[]{:S(2)}) collective-permute-start(f32[1,64,128]{2,1,0:T(8,128)S(1)} %get-tuple-element.151), channel_id=1, source_target_pairs={{0,8},{8,16},{16,24},{1,9},{9,17},{17,25},{2,10},{10,18},{18,26},{... | collective-permute-start | bytes 98312 | tf_op jit(solution)/shard_map/ppermute | solution.py:19
  384.0 5.2 collective-permute-start.3
  387.5 7.0 %collective-permute-start.6 = (f32[66,1,128]{2,1,0:T(1,128)S(1)}, f32[66,1,128]{2,1,0:T(1,128)S(1)}, u32[]{:S(2)}, u32[]{:S(2)}) collective-permute-start(f32[66,1,128]{2,1,0:T(1,128)S(1)} %get-tuple-element.131), channel_id=1, source_target_pairs={{1,0},{2,1},{3,2},{4,3},{5,4},{6,5},{7,6},{0,7},{9,8},{10,9},{11,1... | collective-permute-start | bytes 101384 | tf_op jit(solution)/shard_map/ppermute | solution.py:22
  388.7 5.9 %collective-permute-start.4 = (f32[66,1,128]{2,1,0:T(1,128)S(1)}, f32[66,1,128]{2,1,0:T(1,128)S(1)}, u32[]{:S(2)}, u32[]{:S(2)}) collective-permute-start(f32[66,1,128]{2,1,0:T(1,128)S(1)} %get-tuple-element.132), channel_id=1, source_target_pairs={{0,1},{1,2},{2,3},{3,4},{4,5},{5,6},{6,7},{7,0},{8,9},{9,10},{10,1... | collective-permute-start | bytes 101384 | tf_op jit(solution)/shard_map/ppermute | solution.py:19
  390.4 6.0 %collective-permute-start.5 = (f32[66,1,128]{2,1,0:T(1,128)S(1)}, f32[66,1,128]{2,1,0:T(1,128)S(1)}, u32[]{:S(2)}, u32[]{:S(2)}) collective-permute-start(f32[66,1,128]{2,1,0:T(1,128)S(1)} %get-tuple-element.133), channel_id=1, source_target_pairs={{0,1},{1,2},{2,3},{3,4},{4,5},{5,6},{6,7},{7,0},{8,9},{9,10},{10,1... | collective-permute-start | bytes 101384 | tf_op jit(solution)/shard_map/ppermute | solution.py:19
  402.4 6.4 %collective-permute-start.8 = (f32[1,64,128]{2,1,0:T(8,128)S(1)}, f32[1,64,128]{2,1,0:T(8,128)S(1)}, u32[]{:S(2)}, u32[]{:S(2)}) collective-permute-start(f32[1,64,128]{2,1,0:T(8,128)S(1)} %get-tuple-element.147), channel_id=1, source_target_pairs={{0,8},{8,16},{16,24},{1,9},{9,17},{17,25},{2,10},{10,18},{18,26},{... | collective-permute-start | bytes 98312 | tf_op jit(solution)/shard_map/ppermute | solution.py:19
  406.9 5.2 collective-permute-start.9
  412.2 5.5 %collective-permute-start.10 = (f32[66,1,128]{2,1,0:T(1,128)S(1)}, f32[66,1,128]{2,1,0:T(1,128)S(1)}, u32[]{:S(2)}, u32[]{:S(2)}) collective-permute-start(f32[66,1,128]{2,1,0:T(1,128)S(1)} %get-tuple-element.129), channel_id=1, source_target_pairs={{0,1},{1,2},{2,3},{3,4},{4,5},{5,6},{6,7},{7,0},{8,9},{9,10},{10,1... | collective-permute-start | bytes 101384 | tf_op jit(solution)/shard_map/ppermute | solution.py:19
  424.3 5.2 collective-permute-start.13
  429.6 5.8 %collective-permute-start.14 = (f32[66,1,128]{2,1,0:T(1,128)S(1)}, f32[66,1,128]{2,1,0:T(1,128)S(1)}, u32[]{:S(2)}, u32[]{:S(2)}) collective-permute-start(f32[66,1,128]{2,1,0:T(1,128)S(1)} %get-tuple-element.127), channel_id=1, source_target_pairs={{0,1},{1,2},{2,3},{3,4},{4,5},{5,6},{6,7},{7,0},{8,9},{9,10},{10,1... | collective-permute-start | bytes 101384 | tf_op jit(solution)/shard_map/ppermute | solution.py:19
  429.7 5.7 %collective-permute-start.15 = (f32[66,1,128]{2,1,0:T(1,128)S(1)}, f32[66,1,128]{2,1,0:T(1,128)S(1)}, u32[]{:S(2)}, u32[]{:S(2)}) collective-permute-start(f32[66,1,128]{2,1,0:T(1,128)S(1)} %get-tuple-element.128), channel_id=1, source_target_pairs={{1,0},{2,1},{3,2},{4,3},{5,4},{6,5},{7,6},{0,7},{9,8},{10,9},{11,1... | collective-permute-start | bytes 101384 | tf_op jit(solution)/shard_map/ppermute | solution.py:22
  441.8 5.2 collective-permute-start.17
  447.1 5.9 %collective-permute-start.18 = (f32[66,1,128]{2,1,0:T(1,128)S(1)}, f32[66,1,128]{2,1,0:T(1,128)S(1)}, u32[]{:S(2)}, u32[]{:S(2)}) collective-permute-start(f32[66,1,128]{2,1,0:T(1,128)S(1)} %get-tuple-element.125), channel_id=1, source_target_pairs={{0,1},{1,2},{2,3},{3,4},{4,5},{5,6},{6,7},{7,0},{8,9},{9,10},{10,1... | collective-permute-start | bytes 101384 | tf_op jit(solution)/shard_map/ppermute | solution.py:19
  447.1 5.8 %collective-permute-start.19 = (f32[66,1,128]{2,1,0:T(1,128)S(1)}, f32[66,1,128]{2,1,0:T(1,128)S(1)}, u32[]{:S(2)}, u32[]{:S(2)}) collective-permute-start(f32[66,1,128]{2,1,0:T(1,128)S(1)} %get-tuple-element.126), channel_id=1, source_target_pairs={{1,0},{2,1},{3,2},{4,3},{5,4},{6,5},{7,6},{0,7},{9,8},{10,9},{11,1... | collective-permute-start | bytes 101384 | tf_op jit(solution)/shard_map/ppermute | solution.py:22
  459.2 5.2 collective-permute-start.21
  464.5 5.9 %collective-permute-start.22 = (f32[66,1,128]{2,1,0:T(1,128)S(1)}, f32[66,1,128]{2,1,0:T(1,128)S(1)}, u32[]{:S(2)}, u32[]{:S(2)}) collective-permute-start(f32[66,1,128]{2,1,0:T(1,128)S(1)} %get-tuple-element.123), channel_id=1, source_target_pairs={{0,1},{1,2},{2,3},{3,4},{4,5},{5,6},{6,7},{7,0},{8,9},{9,10},{10,1... | collective-permute-start | bytes 101384 | tf_op jit(solution)/shard_map/ppermute | solution.py:19
  464.6 5.8 %collective-permute-start.23 = (f32[66,1,128]{2,1,0:T(1,128)S(1)}, f32[66,1,128]{2,1,0:T(1,128)S(1)}, u32[]{:S(2)}, u32[]{:S(2)}) collective-permute-start(f32[66,1,128]{2,1,0:T(1,128)S(1)} %get-tuple-element.124), channel_id=1, source_target_pairs={{1,0},{2,1},{3,2},{4,3},{5,4},{6,5},{7,6},{0,7},{9,8},{10,9},{11,1... | collective-permute-start | bytes 101384 | tf_op jit(solution)/shard_map/ppermute | solution.py:22
  476.9 5.2 collective-permute-start.25
  482.2 5.9 %collective-permute-start.26 = (f32[66,1,128]{2,1,0:T(1,128)S(1)}, f32[66,1,128]{2,1,0:T(1,128)S(1)}, u32[]{:S(2)}, u32[]{:S(2)}) collective-permute-start(f32[66,1,128]{2,1,0:T(1,128)S(1)} %get-tuple-element.121), channel_id=1, source_target_pairs={{0,1},{1,2},{2,3},{3,4},{4,5},{5,6},{6,7},{7,0},{8,9},{9,10},{10,1... | collective-permute-start | bytes 101384 | tf_op jit(solution)/shard_map/ppermute | solution.py:19
  482.3 5.8 %collective-permute-start.27 = (f32[66,1,128]{2,1,0:T(1,128)S(1)}, f32[66,1,128]{2,1,0:T(1,128)S(1)}, u32[]{:S(2)}, u32[]{:S(2)}) collective-permute-start(f32[66,1,128]{2,1,0:T(1,128)S(1)} %get-tuple-element.122), channel_id=1, source_target_pairs={{1,0},{2,1},{3,2},{4,3},{5,4},{6,5},{7,6},{0,7},{9,8},{10,9},{11,1... | collective-permute-start | bytes 101384 | tf_op jit(solution)/shard_map/ppermute | solution.py:22
  494.4 5.2 collective-permute-start.29
  499.7 5.9 %collective-permute-start.30 = (f32[66,1,128]{2,1,0:T(1,128)S(1)}, f32[66,1,128]{2,1,0:T(1,128)S(1)}, u32[]{:S(2)}, u32[]{:S(2)}) collective-permute-start(f32[66,1,128]{2,1,0:T(1,128)S(1)} %get-tuple-element.119), channel_id=1, source_target_pairs={{0,1},{1,2},{2,3},{3,4},{4,5},{5,6},{6,7},{7,0},{8,9},{9,10},{10,1... | collective-permute-start | bytes 101384 | tf_op jit(solution)/shard_map/ppermute | solution.py:19
  499.8 5.8 %collective-permute-start.31 = (f32[66,1,128]{2,1,0:T(1,128)S(1)}, f32[66,1,128]{2,1,0:T(1,128)S(1)}, u32[]{:S(2)}, u32[]{:S(2)}) collective-permute-start(f32[66,1,128]{2,1,0:T(1,128)S(1)} %get-tuple-element.120), channel_id=1, source_target_pairs={{1,0},{2,1},{3,2},{4,3},{5,4},{6,5},{7,6},{0,7},{9,8},{10,9},{11,1... | collective-permute-start | bytes 101384 | tf_op jit(solution)/shard_map/ppermute | solution.py:22
  511.9 5.2 collective-permute-start.33
  517.2 5.9 %collective-permute-start.34 = (f32[66,1,128]{2,1,0:T(1,128)S(1)}, f32[66,1,128]{2,1,0:T(1,128)S(1)}, u32[]{:S(2)}, u32[]{:S(2)}) collective-permute-start(f32[66,1,128]{2,1,0:T(1,128)S(1)} %get-tuple-element.117), channel_id=1, source_target_pairs={{0,1},{1,2},{2,3},{3,4},{4,5},{5,6},{6,7},{7,0},{8,9},{9,10},{10,1... | collective-permute-start | bytes 101384 | tf_op jit(solution)/shard_map/ppermute | solution.py:19
  517.3 5.8 %collective-permute-start.35 = (f32[66,1,128]{2,1,0:T(1,128)S(1)}, f32[66,1,128]{2,1,0:T(1,128)S(1)}, u32[]{:S(2)}, u32[]{:S(2)}) collective-permute-start(f32[66,1,128]{2,1,0:T(1,128)S(1)} %get-tuple-element.118), channel_id=1, source_target_pairs={{1,0},{2,1},{3,2},{4,3},{5,4},{6,5},{7,6},{0,7},{9,8},{10,9},{11,1... | collective-permute-start | bytes 101384 | tf_op jit(solution)/shard_map/ppermute | solution.py:22
  (23 other events, 228.5 us)
where the time goes:
time: 536 us; the launch traced here: 528 us
  other arithmetic  301 us (56%)
  starting transfers between devices  99.6 us (19%)
  waiting for transfers between devices  62.5 us (12%)
  local copies, waits for them, and re-layouts  47.3 us (9%)
  loops' own time  16.7 us (3%)
    another operation x16, other arithmetic, evolve(): optical = jnp.cumsum(layer_depth, axis=1)  167 us
    ppermute x18, starting transfers between devices, padded_2(): lax.ppermute(lax.slice_in_dim(block, 0, width, axis=dim), axis, backward)  51.7 us
    reduce_sum x16, other arithmetic, evolve(): layered = jnp.sum(profile[:, :, None] * (transmit_above - transmit), axis=1)  33.4 us
    add x8, other arithmetic, relax(): summed = summed + 0.5 * (kappa_centre + kappa_near) * (neighbour - centre)  32.3 us
    ppermute x18, starting transfers between devices, padded_2(): lax.ppermute(lax.slice_in_dim(block, block.shape[dim] - width, None, axis...  30.6 us
    scatter-add x1, other arithmetic, local(): increment = jnp.zeros((tile_rows * tile_cols, levels), jnp.float32).at[as...  29.5 us
    ppermute x18, waiting for transfers between devices, padded_2(): lax.ppermute(lax.slice_in_dim(block, 0, width, axis=dim), axis, backward)  23.9 us
    another operation x1, loops' own time, local(): lax.map(lambda packed: assess(packed[0], packed[1], packed[2], absorb, se...  16.7 us
  transfers between devices with their start and end apart: 40, of which 21 were waited for; matrix products, arithmetic and copies ran while one was open for 2% of the time, Pallas kernels for 0%

commit v1 on v0

v1 whole, which is shorter than its diff:
```python
import functools
import math

import jax
import jax.numpy as jnp
from jax import lax
from jax.experimental import pallas as pl
from jax.experimental.pallas import tpu as pltpu
from jax.sharding import PartitionSpec as P

STEPS = 8
REJECTED = 64.0
META = 8
LOG2E = math.log2(math.e)
LN2 = math.log(2.0)
VMEM_LIMIT = 60 * 1024 * 1024


def thirds(x):
    high = x.astype(jnp.bfloat16)
    rest = x - high.astype(jnp.float32)
    mid = rest.astype(jnp.bfloat16)
    low = (rest - mid.astype(jnp.float32)).astype(jnp.bfloat16)
    return high, mid, low


def dot_f32(a, b, contract):
    return lax.dot_general(a, b, (contract, ((), ())), preferred_element_type=jnp.float32)


def iota(shape, dim):
    return lax.broadcasted_iota(jnp.int32, shape, dim)


def pack_kernel(
    dev_count, capacity, tile_cols, lane_ref, tile_ref, anchor_ref, weights_ref, observed_ref,
    accept_ref, send_ref, slot_ref, vals_ref
):
    foot_count, channels = observed_ref.shape
    bf16 = jnp.bfloat16
    tile = tile_ref[...]
    onehot = jnp.where(iota((dev_count, foot_count), 0) == tile, 1.0, 0.0)
    earlier = jnp.where(
        iota((foot_count, foot_count), 0) < iota((foot_count, foot_count), 1), 1.0, 0.0
    ).astype(bf16)
    before = dot_f32(onehot.astype(bf16), earlier, ((1,), (0,)))
    rank = jnp.sum(before * onehot, axis=0, keepdims=True).astype(jnp.int32)
    slot = tile * capacity + rank
    slot_ref[...] = slot

    chosen = jnp.where(accept_ref[...] != 0, observed_ref[...], REJECTED)
    parts = thirds(chosen)
    per_chunk = max(1, 128 // capacity)
    chunk = per_chunk * capacity
    for start in range(0, dev_count, per_chunk):
        place = jnp.where(
            iota((chunk, foot_count), 0) + start * capacity == slot, 1.0, 0.0
        ).astype(bf16)
        rows = [dot_f32(place, part, ((1,), (0,))) for part in parts]
        rows = (rows[0] + rows[1]) + rows[2]
        send_ref[start : start + per_chunk, :capacity, :] = rows.reshape(
            per_chunk, capacity, channels
        )

    anchor = anchor_ref[...]
    line = jnp.floor((anchor.astype(jnp.float32) + 0.5) * (1.0 / (tile_cols - 1)))
    base = anchor.astype(jnp.float32) + line
    weights = weights_ref[...]
    shares = weights / jnp.sum(weights, axis=0, keepdims=True)
    meta = jnp.concatenate(
        [base, shares, jnp.zeros((META - 5, foot_count), jnp.float32)], axis=0
    )
    for dev in range(dev_count):
        vals_ref[dev * META : (dev + 1) * META, :] = jnp.where(tile == dev, meta, 0.0)
    lanes = jnp.where(
        iota((channels, foot_count), 0) == rank + lane_ref[0], 1.0, 0.0
    ).astype(bf16)
    rows = [dot_f32(part, lanes, ((1,), (1,))) for part in thirds(vals_ref[...])]
    rows = (rows[0] + rows[1]) + rows[2]
    send_ref[:, capacity:, :] = rows.reshape(dev_count, META, channels)


def column_kernel(
    capacity, halo, recv_ref, recv_any, background_ref, absorb_ref, sensitivity_ref, inverse_ref,
    evolved_ref, field_ref, top_ref, bottom_ref, left_ref, right_ref,
    base_ref, sem, cells_ref, absorb_b, slope_b, inverse_b, taken_ref, profile_ref, rise_ref,
    obs_ref, evo_ref, depth_ref, trans_ref, weigh_ref, slant_ref, sums_ref
):
    dev_count = recv_ref.shape[0]
    tile_rows, tile_cols, levels = background_ref.shape
    cells = tile_rows * tile_cols
    channels = absorb_ref.shape[1]
    lanes = 128
    group = lanes // capacity
    blocks = dev_count // group
    slots = dev_count * capacity
    wide = 32

    copy = pltpu.make_async_copy(recv_any.at[:, capacity, :], base_ref, sem)
    copy.start()

    cells_ref[...] = background_ref[...].reshape(cells, levels).astype(jnp.float32)
    slope_b[...] = jnp.broadcast_to(sensitivity_ref[...] * LOG2E, (lanes, channels)).T
    inverse_b[...] = jnp.broadcast_to(inverse_ref[...], (lanes, channels)).T

    def spread(i, carry):
        turned = (absorb_ref[pl.ds(i * 8, 8), :] * LOG2E).T
        for u in range(8):
            absorb_b[i * 8 + u] = jnp.broadcast_to(turned[:, u : u + 1], (channels, lanes))
        return carry

    lax.fori_loop(0, levels // 8, spread, 0)
    sums_ref[...] = jnp.zeros_like(sums_ref)
    copy.wait()

    def gather(i, carry):
        for u in range(8):
            slot = i * 8 + u
            base = base_ref[lax.div(i * 8, capacity), lax.rem(i * 8, lanes) + u].astype(jnp.int32)
            for k, step in enumerate((0, 1, tile_cols, tile_cols + 1)):
                taken_ref[k, pl.ds(slot, 1), :] = cells_ref[pl.ds(base + step, 1), :]
        return carry

    lax.fori_loop(0, slots // 8, gather, 0)

    def block(f, carry):
        first = pl.multiple_of(f * lanes, lanes)
        mine = recv_ref[pl.ds(f * group, group)]
        shares = jnp.sum(mine[:, capacity:, :], axis=0)
        obs_ref[...] = mine[:, :capacity, :].reshape(lanes, channels).T
        profile = shares[1:2] * taken_ref[0, pl.ds(first, lanes), :].T
        for k in range(1, 4):
            profile = profile + shares[k + 1 : k + 2] * taken_ref[k, pl.ds(first, lanes), :].T
        profile_ref[...] = profile
        rise_ref[0 : levels - 1, :] = profile[1:] - profile[:-1]
        rise_ref[levels - 1 : levels, :] = jnp.zeros((1, lanes), jnp.float32)
        weigh_ref[...] = jnp.zeros_like(weigh_ref)
        slant_ref[...] = jnp.zeros_like(slant_ref)

        def some_channels(c, carry):
            at = pl.multiple_of(c * wide, wide)
            slope = slope_b[pl.ds(at, wide), :]

            def down(i, state):
                path, total = state
                for u in range(8):
                    level = i * 8 + u
                    depth = absorb_b[level, pl.ds(at, wide), :] * jnp.exp2(
                        slope * profile_ref[pl.ds(level, 1), :]
                    )
                    path = path - depth
                    trans = jnp.exp2(path)
                    total = total + trans * rise_ref[pl.ds(level, 1), :]
                    depth_ref[level] = depth
                    trans_ref[level] = trans
                return path, total

            zero = jnp.zeros((wide, lanes), jnp.float32)
            _, total = lax.fori_loop(0, levels // 8, down, (zero, zero))
            evolved = total + profile_ref[0:1, :]
            evo_ref[pl.ds(at, wide), :] = evolved
            obs = obs_ref[pl.ds(at, wide), :]
            force = jnp.where(
                obs < 0.5 * REJECTED, inverse_b[pl.ds(at, wide), :] * (obs - evolved), 0.0
            )
            pull = force * (slope * (LN2 * LN2))

            def up(i, above):
                for u in range(8):
                    level = levels - 1 - (i * 8 + u)
                    trans = trans_ref[level]
                    above = above + (pull * trans) * rise_ref[pl.ds(level, 1), :]
                    weigh = force * trans
                    slant = depth_ref[level] * above
                    weigh_ref[level] += jnp.sum(weigh.reshape(wide // 8, 8, lanes), axis=0)
                    slant_ref[level] += jnp.sum(slant.reshape(wide // 8, 8, lanes), axis=0)
                return above

            lax.fori_loop(0, levels // 8, up, zero)
            return carry

        lax.fori_loop(0, channels // wide, some_channels, 0)
        evolved_ref[pl.ds(f * group, group)] = evo_ref[...].T.reshape(group, capacity, channels)
        weigh = jnp.sum(weigh_ref[...], axis=1)
        slant = jnp.sum(slant_ref[...], axis=1)
        force_all = jnp.zeros((1, lanes), jnp.float32)
        for c in range(channels // wide):
            obs = obs_ref[c * wide : (c + 1) * wide, :]
            force = jnp.where(
                obs < 0.5 * REJECTED,
                inverse_b[c * wide : (c + 1) * wide, :]
                * (obs - evo_ref[c * wide : (c + 1) * wide, :]),
                0.0,
            )
            force_all = force_all + jnp.sum(force, axis=0, keepdims=True)
        over = jnp.concatenate([force_all, weigh[:-1]], axis=0)
        under = jnp.concatenate([weigh[:-1], jnp.zeros((1, lanes), jnp.float32)], axis=0)
        push = (over - under) - slant
        for k in range(4):
            taken_ref[k, pl.ds(first, lanes), :] = (shares[k + 1 : k + 2] * push).T
        return carry

    lax.fori_loop(0, blocks, block, 0)

    def scatter(i, carry):
        for u in range(8):
            slot = i * 8 + u
            base = base_ref[lax.div(i * 8, capacity), lax.rem(i * 8, lanes) + u].astype(jnp.int32)
            for k, step in enumerate((0, 1, tile_cols, tile_cols + 1)):
                sums_ref[k, pl.ds(base + step, 1), :] += taken_ref[k, pl.ds(slot, 1), :]
        return carry

    lax.fori_loop(0, slots // 8, scatter, 0)

    field = (sums_ref[0] + sums_ref[1]) + (sums_ref[2] + sums_ref[3])
    field = field.reshape(tile_rows, tile_cols, levels)
    field_ref[...] = field
    top_ref[...] = field[:halo]
    bottom_ref[...] = field[tile_rows - halo :]
    left_ref[...] = field[:, :halo]
    right_ref[...] = field[:, tile_cols - halo :]


def relax_kernel(
    halo, inside_ref, field_refs, kappa_refs, out_ref, first_ref, second_ref, east_ref, south_ref
):
    tile_rows, tile_cols, levels = out_ref.shape
    height, breadth = tile_rows + 2 * halo, tile_cols + 2 * halo

    def lay(target, refs):
        centre, north, south, west, east, wests, easts = refs
        low, high = slice(0, halo), slice(halo, 2 * halo)
        mid_r, mid_c = slice(halo, halo + tile_rows), slice(halo, halo + tile_cols)
        end_r, end_c = slice(halo + tile_rows, height), slice(halo + tile_cols, breadth)
        target[mid_r, mid_c] = centre[...]
        target[low, mid_c] = north[...]
        target[end_r, mid_c] = south[...]
        target[mid_r, low] = west[...]
        target[mid_r, end_c] = east[...]
        target[low, low] = wests[low]
        target[end_r, low] = wests[high]
        target[low, end_c] = easts[low]
        target[end_r, end_c] = easts[high]

    lay(first_ref, kappa_refs)

    def edges(i, carry):
        here = first_ref[i]
        east_ref[i] = 0.5 * (here + pltpu.roll(here, breadth - 1, 0))
        south_ref[i] = 0.5 * (here + first_ref[i + 1])
        return carry

    lax.fori_loop(0, height - 1, edges, 0)
    lay(first_ref, field_refs)

    source, target = first_ref, second_ref
    for step in range(1, halo + 1):
        last = step == halo

        def row(i, carry, scale=None, source=source, target=target, last=last):
            here, from_north = carry
            below = source[i + 1]
            to_east = east_ref[i] * (pltpu.roll(here, breadth - 1, 0) - here)
            from_south = south_ref[i] * (below - here)
            value = here + (to_east - pltpu.roll(to_east, 1, 0)) + (from_south - from_north)
            if scale is not None:
                value = value * scale
            if last:
                out_ref[i - halo] = value[halo : halo + tile_cols]
            else:
                target[i] = value
            return below, from_south

        here = source[step]
        carry = (here, south_ref[step - 1] * (here - source[step - 1]))
        carry = lax.fori_loop(
            step, halo, functools.partial(row, scale=inside_ref[0]), carry
        )
        carry = lax.fori_loop(halo, halo + tile_rows, row, carry)
        lax.fori_loop(
            halo + tile_rows, height - step, functools.partial(row, scale=inside_ref[1]), carry
        )
        if step == 1:
            target[0] = source[0]
            target[height - 1] = source[height - 1]
        source, target = target, source


def depart_kernel(slot_ref, evolved_ref, observed_ref, out_ref):
    foot_count, _ = observed_ref.shape
    slots = evolved_ref.shape[0]
    slot = slot_ref[...]
    parts = thirds(evolved_ref[...])
    chosen = jnp.where(iota((slots, foot_count), 0) == slot, 1.0, 0.0).astype(jnp.bfloat16)
    rows = [dot_f32(chosen, part, ((0,), (0,))) for part in parts]
    out_ref[...] = observed_ref[...] - ((rows[0] + rows[1]) + rows[2])


def vmem():
    return pl.BlockSpec(memory_space=pltpu.VMEM)


def smem():
    return pl.BlockSpec(memory_space=pltpu.SMEM)


def params():
    return pltpu.CompilerParams(vmem_limit_bytes=VMEM_LIMIT)


def cost(flops, transcendentals, moved):
    return pl.CostEstimate(flops=flops, transcendentals=transcendentals, bytes_accessed=moved)


def neighbours(axis, periodic):
    count = lax.axis_size(axis)
    forward = [(i, i + 1) for i in range(count - 1)]
    if periodic:
        forward.append((count - 1, 0))
    return forward, [(target, source) for source, target in forward]


def halos(top, bottom, left, right):
    lat_up, lat_down = neighbours("lat", False)
    lon_up, lon_down = neighbours("lon", True)
    halo = top.shape[0]
    west = lax.ppermute(right, "lon", lon_up)
    east = lax.ppermute(left, "lon", lon_down)
    north = lax.ppermute(bottom, "lat", lat_up)
    south = lax.ppermute(top, "lat", lat_down)
    wests = lax.ppermute(
        jnp.concatenate([north[:, -halo:], south[:, -halo:]], axis=0), "lon", lon_up
    )
    easts = lax.ppermute(
        jnp.concatenate([north[:, :halo], south[:, :halo]], axis=0), "lon", lon_down
    )
    return north, south, west, east, wests, easts


def local(
    background, diffusivity, tile_index, anchor, weights, observed, accept, absorb, sensitivity,
    inverse_variance
):
    f32 = jnp.float32
    lat_count = lax.axis_size("lat")
    lon_count = lax.axis_size("lon")
    dev_count = lat_count * lon_count
    foot_count, channels = observed.shape
    capacity = max(2, 2 * foot_count // dev_count)
    tile_rows, tile_cols, levels = background.shape
    slots = dev_count * capacity
    lanes = 128
    group = lanes // capacity
    cells = tile_rows * tile_cols
    halo = STEPS

    kappa_halos = halos(
        diffusivity[:halo], diffusivity[-halo:], diffusivity[:, :halo], diffusivity[:, -halo:]
    )

    me = lax.axis_index("lat") * lon_count + lax.axis_index("lon")
    lane = (lax.rem(me, group) * capacity).astype(jnp.int32).reshape(1)
    send, slot = pl.pallas_call(
        functools.partial(pack_kernel, dev_count, capacity, tile_cols),
        out_shape=(
            jax.ShapeDtypeStruct((dev_count, capacity + META, channels), f32),
            jax.ShapeDtypeStruct((1, foot_count), jnp.int32),
        ),
        in_specs=[smem()] + [vmem()] * 5,
        out_specs=(vmem(), vmem()),
        scratch_shapes=[pltpu.VMEM((dev_count * META, foot_count), f32)],
        compiler_params=params(),
        cost_estimate=cost(2 * slots * foot_count * channels * 3, 0, 4 * slots * channels * 3),
        name="pack",
    )(
        lane, tile_index.reshape(1, foot_count), anchor.reshape(1, foot_count), weights.T,
        observed, accept
    )
    recv = lax.all_to_all(send, ("lat", "lon"), split_axis=0, concat_axis=0, tiled=True)

    wide = 32
    evolved, field, top, bottom, left, right = pl.pallas_call(
        functools.partial(column_kernel, capacity, halo),
        out_shape=(
            jax.ShapeDtypeStruct((dev_count, capacity, channels), f32),
            jax.ShapeDtypeStruct((tile_rows, tile_cols, levels), f32),
            jax.ShapeDtypeStruct((halo, tile_cols, levels), f32),
            jax.ShapeDtypeStruct((halo, tile_cols, levels), f32),
            jax.ShapeDtypeStruct((tile_rows, halo, levels), f32),
            jax.ShapeDtypeStruct((tile_rows, halo, levels), f32),
        ),
        in_specs=[vmem(), pl.BlockSpec(memory_space=pl.ANY)] + [vmem()] * 4,
        out_specs=(vmem(),) * 6,
        scratch_shapes=[
            pltpu.SMEM((dev_count, channels), f32),
            pltpu.SemaphoreType.DMA,
            pltpu.VMEM((cells, levels), f32),
            pltpu.VMEM((levels, channels, lanes), f32),
            pltpu.VMEM((channels, lanes), f32),
            pltpu.VMEM((channels, lanes), f32),
            pltpu.VMEM((4, slots, levels), f32),
            pltpu.VMEM((levels, lanes), f32),
            pltpu.VMEM((levels, lanes), f32),
            pltpu.VMEM((channels, lanes), f32),
            pltpu.VMEM((channels, lanes), f32),
            pltpu.VMEM((levels, wide, lanes), f32),
            pltpu.VMEM((levels, wide, lanes), f32),
            pltpu.VMEM((levels, 8, lanes), f32),
            pltpu.VMEM((levels, 8, lanes), f32),
            pltpu.VMEM((4, cells, levels), f32),
        ],
        compiler_params=params(),
        cost_estimate=cost(
            14 * slots * levels * channels, 2 * slots * levels * channels, 12 * cells * levels
        ),
        name="column",
    )(
        recv, recv, background, absorb, sensitivity.reshape(1, channels),
        inverse_variance.reshape(1, channels)
    )

    returned = lax.all_to_all(evolved, ("lat", "lon"), split_axis=0, concat_axis=0, tiled=True)
    field_halos = halos(top, bottom, left, right)

    departure = pl.pallas_call(
        depart_kernel,
        out_shape=jax.ShapeDtypeStruct((foot_count, channels), f32),
        in_specs=[vmem()] * 3,
        out_specs=vmem(),
        compiler_params=params(),
        cost_estimate=cost(2 * slots * foot_count * channels * 3, 0, 4 * slots * channels * 2),
        name="depart",
    )(slot, returned.reshape(slots, channels), observed)

    lat_at = lax.axis_index("lat")
    inside = jnp.stack([lat_at > 0, lat_at < lat_count - 1]).astype(f32)
    height, breadth = tile_rows + 2 * halo, tile_cols + 2 * halo

    def relax_body(inside_ref, *refs):
        relax_kernel(halo, inside_ref, refs[:7], refs[7:14], *refs[14:])

    increment = pl.pallas_call(
        relax_body,
        out_shape=jax.ShapeDtypeStruct((tile_rows, tile_cols, levels), f32),
        in_specs=[smem()] + [vmem()] * 14,
        out_specs=vmem(),
        scratch_shapes=[pltpu.VMEM((height, breadth, levels), f32)] * 4,
        compiler_params=params(),
        cost_estimate=cost(10 * STEPS * height * breadth * levels, 0, 16 * cells * levels),
        name="relax",
    )(inside, field, *field_halos, diffusivity, *kappa_halos)
    return (departure, increment)


def solution(mesh):
    in_specs = (
        P("lat", "lon", None),
        P("lat", "lon", None),
        P(("lat", "lon"), None),
        P(("lat", "lon")),
        P(("lat", "lon"), None),
        P(("lat", "lon"), None),
        P(("lat", "lon"), None),
        P(),
        P(),
        P(),
    )
    out_specs = (P(("lat", "lon"), None), P("lat", "lon", None))
    return jax.shard_map(local, mesh=mesh, in_specs=in_specs, out_specs=out_specs, check_vma=False)
```

time: 536 us -> 165 us (0.31); the launches traced: 528 us -> 165 us
  other arithmetic: 301 us -> 0.62 us
  Pallas kernels: 0 us -> 98.6 us
  starting transfers between devices: 99.6 us -> 34.7 us
  local copies, waits for them, and re-layouts: 47.3 us -> 3.86 us
  waiting for transfers between devices: 62.5 us -> 26.3 us
  loops' own time: 16.7 us -> 0 us
    another operation x21 -> x0, other arithmetic: 168 us -> none  [the longest x16 167 us: evolve(): optical = jnp.cumsum(layer_depth, axis=1)]
    pallas_call x0 -> x4, Pallas kernels: none -> 98.6 us  [the longest x1 74.9 us: local(): pl.pallas_call(functools.partial(column_kernel, capacity, halo), out_shap...]
    ppermute x36 -> x12, starting transfers between devices: 82.3 us -> 25.2 us  [the longest x2 6.97 us: halos(): east = lax.ppermute(left, 'lon', lon_down)]
    reduce_sum x27 -> x0, other arithmetic: 46.2 us -> none  [the longest x16 33.4 us: evolve(): layered = jnp.sum(profile[:, :, None] * (transmit_above - transmit), axis=1)]
    add x10 -> x0, other arithmetic: 33.1 us -> none  [the longest x8 32.3 us: relax(): summed = summed + 0.5 * (kappa_centre + kappa_near) * (neighbour - centre)]
    scatter-add x1 -> x0, other arithmetic: 29.5 us -> none  [local(): increment = jnp.zeros((tile_rows * tile_cols, levels), jnp.float32).at[as...]
    ppermute x36 -> x12, waiting for transfers between devices: 34.4 us -> 14.4 us  [the longest x2 7.56 us: halos(): south = lax.ppermute(top, 'lat', lat_down)]
    another operation x1 -> x0, loops' own time: 16.7 us -> none  [local(): lax.map(lambda packed: assess(packed[0], packed[1], packed[2], absorb, se...]
  transfers between devices with their start and end apart: 40 -> 14, of which waited for: 21 -> 5; matrix products, arithmetic and copies ran while one was open for 2% -> 1% of each run, Pallas kernels for 0% -> 56%
where the time goes in v1:
time: 165 us
  Pallas kernels  98.6 us (60%)
  starting transfers between devices  34.7 us (21%)
  waiting for transfers between devices  26.3 us (16%)
  local copies, waits for them, and re-layouts  3.86 us (2%)
    pallas_call x1, Pallas kernels, local(): pl.pallas_call(functools.partial(column_kernel, capacity, halo), out_shap...  74.9 us
    pallas_call x1, Pallas kernels, local(): pl.pallas_call(relax_body, out_shape=jax.ShapeDtypeStruct((tile_rows, til...  17.3 us
    all_to_all x1, waiting for transfers between devices, local(): lax.all_to_all(send, ('lat', 'lon'), split_axis=0, concat_axis=0, tiled=T...  11.8 us
    ppermute x2, waiting for transfers between devices, halos(): south = lax.ppermute(top, 'lat', lat_down)  7.56 us
    all_to_all x1, starting transfers between devices, local(): lax.all_to_all(send, ('lat', 'lon'), split_axis=0, concat_axis=0, tiled=T...  7.08 us
    ppermute x2, starting transfers between devices, halos(): east = lax.ppermute(left, 'lon', lon_down)  6.97 us
    ppermute x2, waiting for transfers between devices, halos(): lax.ppermute(jnp.concatenate([north[:, :halo], south[:, :halo]], axis=0),...  6.86 us
    ppermute x2, starting transfers between devices, halos(): north = lax.ppermute(bottom, 'lat', lat_up)  6.05 us
  transfers between devices with their start and end apart: 14, of which 5 were waited for; matrix products, arithmetic and copies ran while one was open for 1% of the time, Pallas kernels for 56%

profile of v1, /device:TPU:1, one launch (start us, length us, event | category | flops | bytes accessed | tf_op | source)
XLA Modules:
  0.0 164.9 jit_solution(16754520119098452038)
XLA Ops:
  0.6 0.0 copy-start
  0.7 3.5 %pack.1 = (f32[32,40,128]{2,1,0:T(8,128)}, s32[1,512]{1,0:T(1,128)}) custom-call(s32[1]{0:T(128)} %bitcast.lane_ref, s32[1,512]{1,0:T(1,128)} %bitcast.11, s32[1,512]{1,0:T(1,128)} %bitcast.12, f32[4,512]{1,0:T(4,128)} %bitcast.10, f32[512,128]{1,0:T(8,128)} %observed_ref.3, s32[512,128]{1,0:T(8,128)} %accept_ref.1), custom_call_target="tpu_custom_call" | custom-call | flops 402653184 | bytes 1572864 | tf_op jit(solution)/shard_map/pack/pallas_call | solution.py:363
  4.2 7.1 %all-to-all-start = ((f32[32,40,128]{2,1,0:T(8,128)}), f32[32,40,128]{2,1,0:T(8,128)S(1)}, u32[]{:S(2)}, u32[]{:S(2)}) async-start(f32[32,40,128]{2,1,0:T(8,128)} %get-tuple-element.11), calls=%async_computation | async-start | bytes 1310720 | tf_op jit(solution)/shard_map/all_to_all | solution.py:379
  11.3 0.8 fusion.1
  12.1 2.2 %collective-permute-start.7 = (f32[8,64,128]{2,1,0:T(8,128)}, f32[8,64,128]{2,1,0:T(8,128)S(1)}, u32[]{:S(2)}, u32[]{:S(2)}) collective-permute-start(f32[8,64,128]{2,1,0:T(8,128)} %get-tuple-element.20), channel_id=1, source_target_pairs={{8,0},{16,8},{24,16},{9,1},{17,9},{25,17},{10,2},{18,10},{26,18},{... | collective-permute-start | bytes 786440 | tf_op jit(solution)/shard_map/ppermute | solution.py:330
  14.3 3.4 %collective-permute-start.6 = (f32[8,64,128]{2,1,0:T(8,128)}, f32[8,64,128]{2,1,0:T(8,128)S(1)}, u32[]{:S(2)}, u32[]{:S(2)}) collective-permute-start(f32[8,64,128]{2,1,0:T(8,128)} %get-tuple-element.21), channel_id=1, source_target_pairs={{0,8},{8,16},{16,24},{1,9},{9,17},{17,25},{2,10},{10,18},{18,26},{... | collective-permute-start | bytes 786440 | tf_op jit(solution)/shard_map/ppermute | solution.py:329
  17.7 0.7 fusion
  18.5 4.1 %collective-permute-start.9 = (f32[64,8,128]{2,1,0:T(8,128)}, f32[64,8,128]{2,1,0:T(8,128)S(1)}, u32[]{:S(2)}, u32[]{:S(2)}) collective-permute-start(f32[64,8,128]{2,1,0:T(8,128)} %get-tuple-element.18), channel_id=1, source_target_pairs={{1,0},{2,1},{3,2},{4,3},{5,4},{6,5},{7,6},{0,7},{9,8},{10,9},{11,1... | collective-permute-start | bytes 786440 | tf_op jit(solution)/shard_map/ppermute | solution.py:328
  22.6 1.0 collective-permute-done.7.refs_9_
  23.6 11.8 %all-to-all-done.recv_ref.recv_any = f32[32,40,128]{2,1,0:T(8,128)S(1)} async-done(((f32[32,40,128]{2,1,0:T(8,128)}), f32[32,40,128]{2,1,0:T(8,128)S(1)}, u32[]{:S(2)}, u32[]{:S(2)}) %all-to-all-start) | async-done | bytes 655392 | tf_op jit(solution)/shard_map/all_to_all | solution.py:379
  35.5 0.8 copy-done.1
  36.3 74.9 %column.1 = (f32[32,32,128]{2,1,0:T(8,128)}, f32[64,64,128]{2,1,0:T(8,128)}, f32[8,64,128]{2,1,0:T(8,128)}, f32[8,64,128]{2,1,0:T(8,128)}, f32[64,8,128]{2,1,0:T(8,128)}, /*index=5*/f32[64,8,128]{2,1,0:T(8,128)}) custom-call(f32[32,40,128]{2,1,0:T(8,128)} %copy-done.1, f32[32,40,128]{2,1,0:T(8,128)} %copy-done.1, bf16[64,64,128]{2,1,0:T(8,128)(2,1)} %background_ref.1, ...), custom_call_target="tpu_custom_call" | custom-call | flops 234881024 | bytes 6291456 | tf_op jit(solution)/shard_map/column/pallas_call | solution.py:382
  111.2 2.7 %collective-permute-start = (f32[8,64,128]{2,1,0:T(8,128)}, f32[8,64,128]{2,1,0:T(8,128)S(1)}, u32[]{:S(2)}, u32[]{:S(2)}) collective-permute-start(f32[8,64,128]{2,1,0:T(8,128)} %get-tuple-element.14), channel_id=1, source_target_pairs={{0,8},{8,16},{16,24},{1,9},{9,17},{17,25},{2,10},{10,18},{18,26},{... | collective-permute-start | bytes 786440 | tf_op jit(solution)/shard_map/ppermute | solution.py:329
  113.9 2.4 %all-to-all-start.1 = ((f32[32,32,128]{2,1,0:T(8,128)}), f32[32,32,128]{2,1,0:T(8,128)S(1)}, u32[]{:S(2)}, u32[]{:S(2)}) async-start(f32[32,32,128]{2,1,0:T(8,128)} %get-tuple-element.12), calls=%async_computation.1 | async-start | bytes 1048576 | tf_op jit(solution)/shard_map/all_to_all | solution.py:422
  116.2 1.1 collective-permute-start.10
  117.3 2.6 %collective-permute-start.1 = (f32[8,64,128]{2,1,0:T(8,128)}, f32[8,64,128]{2,1,0:T(8,128)S(1)}, u32[]{:S(2)}, u32[]{:S(2)}) collective-permute-start(f32[8,64,128]{2,1,0:T(8,128)} %get-tuple-element.15), channel_id=1, source_target_pairs={{8,0},{16,8},{24,16},{9,1},{17,9},{25,17},{10,2},{18,10},{26,18},{... | collective-permute-start | bytes 786440 | tf_op jit(solution)/shard_map/ppermute | solution.py:330
  119.9 1.3 collective-permute-start.2
  121.2 6.5 %collective-permute-done.1.refs_2_ = f32[8,64,128]{2,1,0:T(8,128)S(1)} collective-permute-done((f32[8,64,128]{2,1,0:T(8,128)}, f32[8,64,128]{2,1,0:T(8,128)S(1)}, u32[]{:S(2)}, u32[]{:S(2)}) %collective-permute-start.1) | collective-permute-done | bytes 262176 | tf_op jit(solution)/shard_map/ppermute | solution.py:330
  127.7 2.8 %collective-permute-start.3 = (f32[64,8,128]{2,1,0:T(8,128)}, f32[64,8,128]{2,1,0:T(8,128)S(1)}, u32[]{:S(2)}, u32[]{:S(2)}) collective-permute-start(f32[64,8,128]{2,1,0:T(8,128)} %get-tuple-element.17), channel_id=1, source_target_pairs={{1,0},{2,1},{3,2},{4,3},{5,4},{6,5},{7,6},{0,7},{9,8},{10,9},{11,1... | collective-permute-start | bytes 786440 | tf_op jit(solution)/shard_map/ppermute | solution.py:328
  130.6 1.0 collective-permute-start.11
  131.6 0.5 collective-permute-start.4
  132.2 3.6 %collective-permute-start.5 = (f32[16,8,128]{2,1,0:T(8,128)S(1)}, f32[16,8,128]{2,1,0:T(8,128)S(1)}, u32[]{:S(2)}, u32[]{:S(2)}) collective-permute-start(f32[16,8,128]{2,1,0:T(8,128)S(1)} %pad_maximum_fusion.1), channel_id=1, source_target_pairs={{1,0},{2,1},{3,2},{4,3},{5,4},{6,5},{7,6},{0,7},{9,8},{10,9},{11,1... | collective-permute-start | bytes 196616 | tf_op jit(solution)/shard_map/ppermute | solution.py:334
  135.8 0.6 add_convert_fusion.inside_ref
  136.4 6.2 %collective-permute-done.11.refs_13_ = f32[16,8,128]{2,1,0:T(8,128)S(1)} collective-permute-done((f32[16,8,128]{2,1,0:T(8,128)S(1)}, f32[16,8,128]{2,1,0:T(8,128)S(1)}, u32[]{:S(2)}, u32[]{:S(2)}) %collective-permute-start.11) | collective-permute-done | bytes 65568 | tf_op jit(solution)/shard_map/ppermute | solution.py:334
  142.6 0.7 collective-permute-done.5.refs_6_
  143.3 0.0 copy-done.9
  143.4 0.1 copy-done.10
  143.4 0.0 copy-done.13
  143.5 0.5 copy-done.14
  143.9 17.3 %relax.1 = f32[64,64,128]{2,1,0:T(8,128)} custom-call(f32[2]{0:T(128)} %add_convert_fusion.inside_ref, f32[64,64,128]{2,1,0:T(8,128)} %get-tuple-element.13.refs_0_, f32[8,64,128]{2,1,0:T(8,128)} %copy-done.5, f32[8,64,128]{2,1,0:T(8,128)} %copy-done.6, f32[64,8,128]{2,1,0:T(8,128)} %copy-done.9, f32[64,8,128]{2,1,0:T(8,128)} %copy-done.10, ...), custom_call_target="tpu_custom_call" | custom-call | flops 65536000 | bytes 8388608 | tf_op jit(solution)/shard_map/relax/pallas_call | solution.py:442
  161.2 0.8 copy-done.2
  162.0 2.9 %depart.1 = f32[512,128]{1,0:T(8,128)} custom-call(s32[1,512]{1,0:T(1,128)} %get-tuple-element.10.slot_ref, f32[1024,128]{1,0:T(8,128)} %bitcast.9, f32[512,128]{1,0:T(8,128)} %observed_ref.3), custom_call_target="tpu_custom_call" | custom-call | flops 402653184 | bytes 1048576 | tf_op jit(solution)/shard_map/depart/pallas_call | solution.py:425
  (41 shorter events, 0.1 us)
Async XLA Ops:
  0.6 10.7 %copy-start = (f32[64,64,128]{2,1,0:T(8,128)S(1)}, f32[64,64,128]{2,1,0:T(8,128)}, u32[]{:S(2)}) copy-start(f32[64,64,128]{2,1,0:T(8,128)} %refs_7_.1) | copy-start | bytes 6291460
  4.2 31.3 %all-to-all-start = ((f32[32,40,128]{2,1,0:T(8,128)}), f32[32,40,128]{2,1,0:T(8,128)S(1)}, u32[]{:S(2)}, u32[]{:S(2)}) async-start(f32[32,40,128]{2,1,0:T(8,128)} %get-tuple-element.11), calls=%async_computation | async-start | bytes 1310720 | tf_op jit(solution)/shard_map/all_to_all | solution.py:379
  12.1 11.5 %collective-permute-start.7 = (f32[8,64,128]{2,1,0:T(8,128)}, f32[8,64,128]{2,1,0:T(8,128)S(1)}, u32[]{:S(2)}, u32[]{:S(2)}) collective-permute-start(f32[8,64,128]{2,1,0:T(8,128)} %get-tuple-element.20), channel_id=1, source_target_pairs={{8,0},{16,8},{24,16},{9,1},{17,9},{25,17},{10,2},{18,10},{26,18},{... | collective-permute-start | bytes 786440 | tf_op jit(solution)/shard_map/ppermute | solution.py:330
  14.3 99.5 %collective-permute-start.6 = (f32[8,64,128]{2,1,0:T(8,128)}, f32[8,64,128]{2,1,0:T(8,128)S(1)}, u32[]{:S(2)}, u32[]{:S(2)}) collective-permute-start(f32[8,64,128]{2,1,0:T(8,128)} %get-tuple-element.21), channel_id=1, source_target_pairs={{0,8},{8,16},{16,24},{1,9},{9,17},{17,25},{2,10},{10,18},{18,26},{... | collective-permute-start | bytes 786440 | tf_op jit(solution)/shard_map/ppermute | solution.py:329
  18.5 112.2 %collective-permute-start.9 = (f32[64,8,128]{2,1,0:T(8,128)}, f32[64,8,128]{2,1,0:T(8,128)S(1)}, u32[]{:S(2)}, u32[]{:S(2)}) collective-permute-start(f32[64,8,128]{2,1,0:T(8,128)} %get-tuple-element.18), channel_id=1, source_target_pairs={{1,0},{2,1},{3,2},{4,3},{5,4},{6,5},{7,6},{0,7},{9,8},{10,9},{11,1... | collective-permute-start | bytes 786440 | tf_op jit(solution)/shard_map/ppermute | solution.py:328
  22.6 109.0 %collective-permute-start.8 = (f32[64,8,128]{2,1,0:T(8,128)S(1)}, f32[64,8,128]{2,1,0:T(8,128)S(1)}, u32[]{:S(2)}, u32[]{:S(2)}) collective-permute-start(f32[64,8,128]{2,1,0:T(8,128)S(1)} %get-tuple-element.19), channel_id=1, source_target_pairs={{0,1},{1,2},{2,3},{3,4},{4,5},{5,6},{6,7},{7,0},{8,9},{9,10},{10,1... | collective-permute-start | bytes 786440 | tf_op jit(solution)/shard_map/ppermute | solution.py:327
  23.6 87.5 %copy-start.3 = (f32[8,64,128]{2,1,0:T(8,128)}, f32[8,64,128]{2,1,0:T(8,128)S(1)}, u32[]{:S(2)}) copy-start(f32[8,64,128]{2,1,0:T(8,128)S(1)} %collective-permute-done.7.refs_9_) | copy-start | bytes 786436
  35.4 0.8 copy-start.1
  111.2 8.7 %collective-permute-start = (f32[8,64,128]{2,1,0:T(8,128)}, f32[8,64,128]{2,1,0:T(8,128)S(1)}, u32[]{:S(2)}, u32[]{:S(2)}) collective-permute-start(f32[8,64,128]{2,1,0:T(8,128)} %get-tuple-element.14), channel_id=1, source_target_pairs={{0,8},{8,16},{16,24},{1,9},{9,17},{17,25},{2,10},{10,18},{18,26},{... | collective-permute-start | bytes 786440 | tf_op jit(solution)/shard_map/ppermute | solution.py:329
  113.8 29.5 %copy-start.4 = (f32[8,64,128]{2,1,0:T(8,128)}, f32[8,64,128]{2,1,0:T(8,128)S(1)}, u32[]{:S(2)}) copy-start(f32[8,64,128]{2,1,0:T(8,128)S(1)} %collective-permute-done.6.refs_8_) | copy-start | bytes 786436
  113.9 47.3 %all-to-all-start.1 = ((f32[32,32,128]{2,1,0:T(8,128)}), f32[32,32,128]{2,1,0:T(8,128)S(1)}, u32[]{:S(2)}, u32[]{:S(2)}) async-start(f32[32,32,128]{2,1,0:T(8,128)} %get-tuple-element.12), calls=%async_computation.1 | async-start | bytes 1048576 | tf_op jit(solution)/shard_map/all_to_all | solution.py:422
  116.2 15.9 %collective-permute-start.10 = (f32[16,8,128]{2,1,0:T(8,128)S(1)}, f32[16,8,128]{2,1,0:T(8,128)S(1)}, u32[]{:S(2)}, u32[]{:S(2)}) collective-permute-start(f32[16,8,128]{2,1,0:T(8,128)S(1)} %pad_maximum_fusion.2), channel_id=1, source_target_pairs={{0,1},{1,2},{2,3},{3,4},{4,5},{5,6},{6,7},{7,0},{8,9},{9,10},{10,1... | collective-permute-start | bytes 196616 | tf_op jit(solution)/shard_map/ppermute | solution.py:331
  117.3 10.4 %collective-permute-start.1 = (f32[8,64,128]{2,1,0:T(8,128)}, f32[8,64,128]{2,1,0:T(8,128)S(1)}, u32[]{:S(2)}, u32[]{:S(2)}) collective-permute-start(f32[8,64,128]{2,1,0:T(8,128)} %get-tuple-element.15), channel_id=1, source_target_pairs={{8,0},{16,8},{24,16},{9,1},{17,9},{25,17},{10,2},{18,10},{26,18},{... | collective-permute-start | bytes 786440 | tf_op jit(solution)/shard_map/ppermute | solution.py:330
  119.9 23.4 %copy-start.5 = (f32[8,64,128]{2,1,0:T(8,128)}, f32[8,64,128]{2,1,0:T(8,128)S(1)}, u32[]{:S(2)}) copy-start(f32[8,64,128]{2,1,0:T(8,128)S(1)} %collective-permute-done.refs_1_) | copy-start | bytes 786436
  119.9 22.7 %collective-permute-start.2 = (f32[64,8,128]{2,1,0:T(8,128)}, f32[64,8,128]{2,1,0:T(8,128)S(1)}, u32[]{:S(2)}, u32[]{:S(2)}) collective-permute-start(f32[64,8,128]{2,1,0:T(8,128)} %get-tuple-element.16), channel_id=1, source_target_pairs={{0,1},{1,2},{2,3},{3,4},{4,5},{5,6},{6,7},{7,0},{8,9},{9,10},{10,1... | collective-permute-start | bytes 786440 | tf_op jit(solution)/shard_map/ppermute | solution.py:327
  127.7 15.6 %copy-start.6 = (f32[8,64,128]{2,1,0:T(8,128)}, f32[8,64,128]{2,1,0:T(8,128)S(1)}, u32[]{:S(2)}) copy-start(f32[8,64,128]{2,1,0:T(8,128)S(1)} %collective-permute-done.1.refs_2_) | copy-start | bytes 786436
  127.7 14.9 %collective-permute-start.3 = (f32[64,8,128]{2,1,0:T(8,128)}, f32[64,8,128]{2,1,0:T(8,128)S(1)}, u32[]{:S(2)}, u32[]{:S(2)}) collective-permute-start(f32[64,8,128]{2,1,0:T(8,128)} %get-tuple-element.17), channel_id=1, source_target_pairs={{1,0},{2,1},{3,2},{4,3},{5,4},{6,5},{7,6},{0,7},{9,8},{10,9},{11,1... | collective-permute-start | bytes 786440 | tf_op jit(solution)/shard_map/ppermute | solution.py:328
  130.6 12.7 %copy-start.7 = (f32[64,8,128]{2,1,0:T(8,128)}, f32[64,8,128]{2,1,0:T(8,128)S(1)}, u32[]{:S(2)}) copy-start(f32[64,8,128]{2,1,0:T(8,128)S(1)} %collective-permute-done.9.refs_11_) | copy-start | bytes 786436
  130.6 12.0 %collective-permute-start.11 = (f32[16,8,128]{2,1,0:T(8,128)S(1)}, f32[16,8,128]{2,1,0:T(8,128)S(1)}, u32[]{:S(2)}, u32[]{:S(2)}) collective-permute-start(f32[16,8,128]{2,1,0:T(8,128)S(1)} %pad_maximum_fusion.3), channel_id=1, source_target_pairs={{1,0},{2,1},{3,2},{4,3},{5,4},{6,5},{7,6},{0,7},{9,8},{10,9},{11,1... | collective-permute-start | bytes 196616 | tf_op jit(solution)/shard_map/ppermute | solution.py:334
  131.6 11.7 %copy-start.8 = (f32[64,8,128]{2,1,0:T(8,128)}, f32[64,8,128]{2,1,0:T(8,128)S(1)}, u32[]{:S(2)}) copy-start(f32[64,8,128]{2,1,0:T(8,128)S(1)} %collective-permute-done.8.refs_10_) | copy-start | bytes 786436
  131.6 11.0 %collective-permute-start.4 = (f32[16,8,128]{2,1,0:T(8,128)S(1)}, f32[16,8,128]{2,1,0:T(8,128)S(1)}, u32[]{:S(2)}, u32[]{:S(2)}) collective-permute-start(f32[16,8,128]{2,1,0:T(8,128)S(1)} %pad_maximum_fusion), channel_id=1, source_target_pairs={{0,1},{1,2},{2,3},{3,4},{4,5},{5,6},{6,7},{7,0},{8,9},{9,10},{10,1... | collective-permute-start | bytes 196616 | tf_op jit(solution)/shard_map/ppermute | solution.py:331
  132.2 11.2 %copy-start.11 = (f32[16,8,128]{2,1,0:T(8,128)}, f32[16,8,128]{2,1,0:T(8,128)S(1)}, u32[]{:S(2)}) copy-start(f32[16,8,128]{2,1,0:T(8,128)S(1)} %collective-permute-done.10.refs_12_) | copy-start | bytes 196612
  132.2 11.1 %collective-permute-start.5 = (f32[16,8,128]{2,1,0:T(8,128)S(1)}, f32[16,8,128]{2,1,0:T(8,128)S(1)}, u32[]{:S(2)}, u32[]{:S(2)}) collective-permute-start(f32[16,8,128]{2,1,0:T(8,128)S(1)} %pad_maximum_fusion.1), channel_id=1, source_target_pairs={{1,0},{2,1},{3,2},{4,3},{5,4},{6,5},{7,6},{0,7},{9,8},{10,9},{11,1... | collective-permute-start | bytes 196616 | tf_op jit(solution)/shard_map/ppermute | solution.py:334
  142.6 0.7 copy-start.12
  142.6 0.8 copy-start.9
  142.6 0.8 copy-start.10
  142.6 0.8 copy-start.13
  143.3 0.6 copy-start.14
  161.2 0.8 copy-start.2

commit v2 on v1

--- a/solution.py
+++ b/solution.py
@@ -13,7 +13,8 @@
 META = 8
 LOG2E = math.log2(math.e)
 LN2 = math.log(2.0)
-VMEM_LIMIT = 60 * 1024 * 1024
+MIB = 1024 * 1024
+UNROLL = 16
 
 
 def thirds(x):
@@ -81,10 +82,10 @@
 
 
 def column_kernel(
-    capacity, halo, recv_ref, recv_any, background_ref, absorb_ref, sensitivity_ref, inverse_ref,
+    capacity, halo, recv_ref, background_ref, absorb_ref, sensitivity_ref, inverse_ref,
     evolved_ref, field_ref, top_ref, bottom_ref, left_ref, right_ref,
-    base_ref, sem, cells_ref, absorb_b, slope_b, inverse_b, taken_ref, profile_ref, rise_ref,
-    obs_ref, evo_ref, depth_ref, trans_ref, weigh_ref, slant_ref, sums_ref
+    base_ref, sem, cells_ref, absorb_b, slope_b, inverse_b, taken_ref, terms_ref, profile_ref,
+    rise_ref, obs_ref, evo_ref, main_ref, side_ref, push_ref, sums_ref
 ):
     dev_count = recv_ref.shape[0]
     tile_rows, tile_cols, levels = background_ref.shape
@@ -93,10 +94,11 @@
     lanes = 128
     group = lanes // capacity
     blocks = dev_count // group
-    slots = dev_count * capacity
-    wide = 32
-
-    copy = pltpu.make_async_copy(recv_any.at[:, capacity, :], base_ref, sem)
+    wide = main_ref.shape[1]
+    per_loop = UNROLL * wide * lanes // (levels * channels)
+    corners = (0, 1, tile_cols, tile_cols + 1)
+
+    copy = pltpu.make_async_copy(recv_ref.at[:, capacity, :], base_ref, sem)
     copy.start()
 
     cells_ref[...] = background_ref[...].reshape(cells, levels).astype(jnp.float32)
@@ -111,106 +113,107 @@
 
     lax.fori_loop(0, levels // 8, spread, 0)
     sums_ref[...] = jnp.zeros_like(sums_ref)
+    terms_ref[...] = jnp.zeros_like(terms_ref)
     copy.wait()
 
-    def gather(i, carry):
+    def base_of(f, at):
+        return base_ref[f * group + lax.div(at, capacity), at].astype(jnp.int32)
+
+    def gather(f, at):
+        base = base_of(f, at)
+        for k, step in enumerate(corners):
+            taken_ref[k, pl.ds(at, 1), :] = cells_ref[pl.ds(base + step, 1), :]
+
+    def scatter(f, at):
+        base = base_of(f, at)
+        for k, step in enumerate(corners):
+            sums_ref[k, pl.ds(base + step, 1), :] += terms_ref[k, pl.ds(at, 1), :]
+
+    def gather_first(i, carry):
         for u in range(8):
-            slot = i * 8 + u
-            base = base_ref[lax.div(i * 8, capacity), lax.rem(i * 8, lanes) + u].astype(jnp.int32)
-            for k, step in enumerate((0, 1, tile_cols, tile_cols + 1)):
-                taken_ref[k, pl.ds(slot, 1), :] = cells_ref[pl.ds(base + step, 1), :]
+            gather(0, i * 8 + u)
         return carry
 
-    lax.fori_loop(0, slots // 8, gather, 0)
+    lax.fori_loop(0, lanes // 8, gather_first, 0)
 
     def block(f, carry):
-        first = pl.multiple_of(f * lanes, lanes)
+        before = jnp.maximum(f - 1, 0)
+        after = jnp.minimum(f + 1, blocks - 1)
         mine = recv_ref[pl.ds(f * group, group)]
         shares = jnp.sum(mine[:, capacity:, :], axis=0)
         obs_ref[...] = mine[:, :capacity, :].reshape(lanes, channels).T
-        profile = shares[1:2] * taken_ref[0, pl.ds(first, lanes), :].T
+        profile = shares[1:2] * taken_ref[0].T
         for k in range(1, 4):
-            profile = profile + shares[k + 1 : k + 2] * taken_ref[k, pl.ds(first, lanes), :].T
+            profile = profile + shares[k + 1 : k + 2] * taken_ref[k].T
         profile_ref[...] = profile
         rise_ref[0 : levels - 1, :] = profile[1:] - profile[:-1]
         rise_ref[levels - 1 : levels, :] = jnp.zeros((1, lanes), jnp.float32)
-        weigh_ref[...] = jnp.zeros_like(weigh_ref)
-        slant_ref[...] = jnp.zeros_like(slant_ref)
+        push_ref[...] = jnp.zeros_like(push_ref)
 
         def some_channels(c, carry):
             at = pl.multiple_of(c * wide, wide)
             slope = slope_b[pl.ds(at, wide), :]
+            scale = slope * (LN2 * LN2)
 
             def down(i, state):
-                path, total = state
-                for u in range(8):
-                    level = i * 8 + u
+                path, total, above = state
+                for u in range(UNROLL):
+                    level = i * UNROLL + u
                     depth = absorb_b[level, pl.ds(at, wide), :] * jnp.exp2(
                         slope * profile_ref[pl.ds(level, 1), :]
                     )
                     path = path - depth
                     trans = jnp.exp2(path)
+                    side = depth * scale
+                    side_ref[level] = side
+                    main_ref[level] = (above - trans) + side * total
                     total = total + trans * rise_ref[pl.ds(level, 1), :]
-                    depth_ref[level] = depth
-                    trans_ref[level] = trans
-                return path, total
+                    above = trans
+                for u in range(per_loop):
+                    scatter(before, (c * (levels // UNROLL) + i) * per_loop + u)
+                return path, total, above
 
             zero = jnp.zeros((wide, lanes), jnp.float32)
-            _, total = lax.fori_loop(0, levels // 8, down, (zero, zero))
+            _, total, last = lax.fori_loop(0, levels // UNROLL, down, (zero, zero, zero + 1.0))
+            main_ref[levels - 1] += last
             evolved = total + profile_ref[0:1, :]
             evo_ref[pl.ds(at, wide), :] = evolved
             obs = obs_ref[pl.ds(at, wide), :]
             force = jnp.where(
                 obs < 0.5 * REJECTED, inverse_b[pl.ds(at, wide), :] * (obs - evolved), 0.0
             )
-            pull = force * (slope * (LN2 * LN2))
-
-            def up(i, above):
-                for u in range(8):
-                    level = levels - 1 - (i * 8 + u)
-                    trans = trans_ref[level]
-                    above = above + (pull * trans) * rise_ref[pl.ds(level, 1), :]
-                    weigh = force * trans
-                    slant = depth_ref[level] * above
-                    weigh_ref[level] += jnp.sum(weigh.reshape(wide // 8, 8, lanes), axis=0)
-                    slant_ref[level] += jnp.sum(slant.reshape(wide // 8, 8, lanes), axis=0)
-                return above
-
-            lax.fori_loop(0, levels // 8, up, zero)
+
+            def up(i, carry):
+                for u in range(UNROLL):
+                    level = i * UNROLL + u
+                    push = force * (main_ref[level] - total * side_ref[level])
+                    push_ref[pl.ds(pl.multiple_of(level * 8, 8), 8), :] += jnp.sum(
+                        push.reshape(wide // 8, 8, lanes), axis=0
+                    )
+                for u in range(per_loop):
+                    gather(after, (c * (levels // UNROLL) + i) * per_loop + u)
+                return carry
+
+            lax.fori_loop(0, levels // UNROLL, up, 0)
             return carry
 
         lax.fori_loop(0, channels // wide, some_channels, 0)
         evolved_ref[pl.ds(f * group, group)] = evo_ref[...].T.reshape(group, capacity, channels)
-        weigh = jnp.sum(weigh_ref[...], axis=1)
-        slant = jnp.sum(slant_ref[...], axis=1)
-        force_all = jnp.zeros((1, lanes), jnp.float32)
-        for c in range(channels // wide):
-            obs = obs_ref[c * wide : (c + 1) * wide, :]
-            force = jnp.where(
-                obs < 0.5 * REJECTED,
-                inverse_b[c * wide : (c + 1) * wide, :]
-                * (obs - evo_ref[c * wide : (c + 1) * wide, :]),
-                0.0,
-            )
-            force_all = force_all + jnp.sum(force, axis=0, keepdims=True)
-        over = jnp.concatenate([force_all, weigh[:-1]], axis=0)
-        under = jnp.concatenate([weigh[:-1], jnp.zeros((1, lanes), jnp.float32)], axis=0)
-        push = (over - under) - slant
+        push = push_ref[pl.ds(0, levels, stride=8), :]
+        for u in range(1, 8):
+            push = push + push_ref[pl.ds(u, levels, stride=8), :]
         for k in range(4):
-            taken_ref[k, pl.ds(first, lanes), :] = (shares[k + 1 : k + 2] * push).T
+            terms_ref[k] = (shares[k + 1 : k + 2] * push).T
         return carry
 
     lax.fori_loop(0, blocks, block, 0)
 
-    def scatter(i, carry):
+    def scatter_last(i, carry):
         for u in range(8):
-            slot = i * 8 + u
-            base = base_ref[lax.div(i * 8, capacity), lax.rem(i * 8, lanes) + u].astype(jnp.int32)
-            for k, step in enumerate((0, 1, tile_cols, tile_cols + 1)):
-                sums_ref[k, pl.ds(base + step, 1), :] += taken_ref[k, pl.ds(slot, 1), :]
+            scatter(blocks - 1, i * 8 + u)
         return carry
 
-    lax.fori_loop(0, slots // 8, scatter, 0)
+    lax.fori_loop(0, lanes // 8, scatter_last, 0)
 
     field = (sums_ref[0] + sums_ref[1]) + (sums_ref[2] + sums_ref[3])
     field = field.reshape(tile_rows, tile_cols, levels)
@@ -221,37 +224,65 @@
     right_ref[...] = field[:, tile_cols - halo :]
 
 
+def lay(halo, target, refs):
+    centre, north, south, west, east, wests, easts = refs
+    tile_rows, tile_cols, _ = centre.shape
+    height, breadth = tile_rows + 2 * halo, tile_cols + 2 * halo
+    low, high = slice(0, halo), slice(halo, 2 * halo)
+    mid_r, mid_c = slice(halo, halo + tile_rows), slice(halo, halo + tile_cols)
+    end_r, end_c = slice(halo + tile_rows, height), slice(halo + tile_cols, breadth)
+    target[mid_r, mid_c] = centre[...]
+    target[low, mid_c] = north[...]
+    target[end_r, mid_c] = south[...]
+    target[mid_r, low] = west[...]
+    target[mid_r, end_c] = east[...]
+    target[low, low] = wests[low]
+    target[end_r, low] = wests[high]
+    target[low, end_c] = easts[low]
+    target[end_r, end_c] = easts[high]
+
+
+def interleave(plain_ref, target_ref):
+    stretch = target_ref.shape[1]
+
+    def row(i, carry):
+        for t in range(stretch):
+            target_ref[i, t] = plain_ref[i, pl.ds(t, 8, stride=stretch), :]
+        return carry
+
+    lax.fori_loop(0, plain_ref.shape[0], row, 0)
+
+
+def eastward(x):
+    return jnp.concatenate([x[1:], pltpu.roll(x[0], 7, 0)[None]], axis=0)
+
+
+def westward(x):
+    return jnp.concatenate([pltpu.roll(x[-1], 1, 0)[None], x[:-1]], axis=0)
+
+
+def edges_kernel(halo, kappa_refs, east_ref, south_ref, plain_ref, kappa_ref):
+    lay(halo, plain_ref, kappa_refs)
+    interleave(plain_ref, kappa_ref)
+    height = plain_ref.shape[0]
+
+    def edges(i, carry):
+        here = kappa_ref[i]
+        east_ref[i] = 0.5 * (here + eastward(here))
+        south_ref[i] = 0.5 * (here + kappa_ref[jnp.minimum(i + 1, height - 1)])
+        return carry
+
+    lax.fori_loop(0, height, edges, 0)
+
+
 def relax_kernel(
-    halo, inside_ref, field_refs, kappa_refs, out_ref, first_ref, second_ref, east_ref, south_ref
+    halo, inside_ref, field_refs, east_ref, south_ref, out_ref, plain_ref, first_ref, second_ref
 ):
     tile_rows, tile_cols, levels = out_ref.shape
-    height, breadth = tile_rows + 2 * halo, tile_cols + 2 * halo
-
-    def lay(target, refs):
-        centre, north, south, west, east, wests, easts = refs
-        low, high = slice(0, halo), slice(halo, 2 * halo)
-        mid_r, mid_c = slice(halo, halo + tile_rows), slice(halo, halo + tile_cols)
-        end_r, end_c = slice(halo + tile_rows, height), slice(halo + tile_cols, breadth)
-        target[mid_r, mid_c] = centre[...]
-        target[low, mid_c] = north[...]
-        target[end_r, mid_c] = south[...]
-        target[mid_r, low] = west[...]
-        target[mid_r, end_c] = east[...]
-        target[low, low] = wests[low]
-        target[end_r, low] = wests[high]
-        target[low, end_c] = easts[low]
-        target[end_r, end_c] = easts[high]
-
-    lay(first_ref, kappa_refs)
-
-    def edges(i, carry):
-        here = first_ref[i]
-        east_ref[i] = 0.5 * (here + pltpu.roll(here, breadth - 1, 0))
-        south_ref[i] = 0.5 * (here + first_ref[i + 1])
-        return carry
-
-    lax.fori_loop(0, height - 1, edges, 0)
-    lay(first_ref, field_refs)
+    height = tile_rows + 2 * halo
+    stretch = first_ref.shape[1]
+    lay(halo, plain_ref, field_refs)
+    interleave(plain_ref, first_ref)
 
     source, target = first_ref, second_ref
     for step in range(1, halo + 1):
@@ -260,13 +291,14 @@
         def row(i, carry, scale=None, source=source, target=target, last=last):
             here, from_north = carry
             below = source[i + 1]
-            to_east = east_ref[i] * (pltpu.roll(here, breadth - 1, 0) - here)
+            to_east = east_ref[i] * (eastward(here) - here)
             from_south = south_ref[i] * (below - here)
-            value = here + (to_east - pltpu.roll(to_east, 1, 0)) + (from_south - from_north)
+            value = here + (to_east - westward(to_east)) + (from_south - from_north)
             if scale is not None:
                 value = value * scale
             if last:
-                out_ref[i - halo] = value[halo : halo + tile_cols]
+                for t in range(stretch):
+                    plain_ref[i, pl.ds(t, 8, stride=stretch), :] = value[t]
             else:
                 target[i] = value
             return below, from_south
@@ -274,16 +306,15 @@
         here = source[step]
         carry = (here, south_ref[step - 1] * (here - source[step - 1]))
         carry = lax.fori_loop(
-            step, halo, functools.partial(row, scale=inside_ref[0]), carry
+            step, halo, functools.partial(row, scale=inside_ref[0]), carry, unroll=True
         )
-        carry = lax.fori_loop(halo, halo + tile_rows, row, carry)
+        carry = lax.fori_loop(halo, halo + tile_rows, row, carry, unroll=4)
         lax.fori_loop(
-            halo + tile_rows, height - step, functools.partial(row, scale=inside_ref[1]), carry
+            halo + tile_rows, height - step, functools.partial(row, scale=inside_ref[1]), carry,
+            unroll=True,
         )
-        if step == 1:
-            target[0] = source[0]
-            target[height - 1] = source[height - 1]
         source, target = target, source
+    out_ref[...] = plain_ref[halo : halo + tile_rows, halo : halo + tile_cols, :]
 
 
 def depart_kernel(slot_ref, evolved_ref, observed_ref, out_ref):
@@ -304,8 +335,8 @@
     return pl.BlockSpec(memory_space=pltpu.SMEM)
 
 
-def params():
-    return pltpu.CompilerParams(vmem_limit_bytes=VMEM_LIMIT)
+def params(mib):
+    return pltpu.CompilerParams(vmem_limit_bytes=mib * MIB)
 
 
 def cost(flops, transcendentals, moved):
@@ -354,10 +385,6 @@
     cells = tile_rows * tile_cols
     halo = STEPS
 
-    kappa_halos = halos(
-        diffusivity[:halo], diffusivity[-halo:], diffusivity[:, :halo], diffusivity[:, -halo:]
-    )
-
     me = lax.axis_index("lat") * lon_count + lax.axis_index("lon")
     lane = (lax.rem(me, group) * capacity).astype(jnp.int32).reshape(1)
     send, slot = pl.pallas_call(
@@ -369,7 +396,7 @@
         in_specs=[smem()] + [vmem()] * 5,
         out_specs=(vmem(), vmem()),
         scratch_shapes=[pltpu.VMEM((dev_count * META, foot_count), f32)],
-        compiler_params=params(),
+        compiler_params=params(16),
         cost_estimate=cost(2 * slots * foot_count * channels * 3, 0, 4 * slots * channels * 3),
         name="pack",
     )(
@@ -377,6 +404,12 @@
         observed, accept
     )
     recv = lax.all_to_all(send, ("lat", "lon"), split_axis=0, concat_axis=0, tiled=True)
+
+    recv, *strips = lax.optimization_barrier((
+        recv, diffusivity[:halo], diffusivity[-halo:], diffusivity[:, :halo],
+        diffusivity[:, -halo:]
+    ))
+    kappa_halos = halos(*strips)
 
     wide = 32
     evolved, field, top, bottom, left, right = pl.pallas_call(
@@ -389,7 +422,7 @@
             jax.ShapeDtypeStruct((tile_rows, halo, levels), f32),
             jax.ShapeDtypeStruct((tile_rows, halo, levels), f32),
         ),
-        in_specs=[vmem(), pl.BlockSpec(memory_space=pl.ANY)] + [vmem()] * 4,
+        in_specs=[vmem()] * 5,
         out_specs=(vmem(),) * 6,
         scratch_shapes=[
             pltpu.SMEM((dev_count, channels), f32),
@@ -398,24 +431,24 @@
             pltpu.VMEM((levels, channels, lanes), f32),
             pltpu.VMEM((channels, lanes), f32),
             pltpu.VMEM((channels, lanes), f32),
-            pltpu.VMEM((4, slots, levels), f32),
+            pltpu.VMEM((4, lanes, levels), f32),
+            pltpu.VMEM((4, lanes, levels), f32),
             pltpu.VMEM((levels, lanes), f32),
             pltpu.VMEM((levels, lanes), f32),
             pltpu.VMEM((channels, lanes), f32),
             pltpu.VMEM((channels, lanes), f32),
             pltpu.VMEM((levels, wide, lanes), f32),
             pltpu.VMEM((levels, wide, lanes), f32),
-            pltpu.VMEM((levels, 8, lanes), f32),
-            pltpu.VMEM((levels, 8, lanes), f32),
+            pltpu.VMEM((levels * 8, lanes), f32),
             pltpu.VMEM((4, cells, levels), f32),
         ],
-        compiler_params=params(),
+        compiler_params=params(60),
         cost_estimate=cost(
             14 * slots * levels * channels, 2 * slots * levels * channels, 12 * cells * levels
         ),
         name="column",
     )(
-        recv, recv, background, absorb, sensitivity.reshape(1, channels),
+        recv, background, absorb, sensitivity.reshape(1, channels),
         inverse_variance.reshape(1, channels)
     )
 
@@ -427,7 +460,7 @@
         out_shape=jax.ShapeDtypeStruct((foot_count, channels), f32),
         in_specs=[vmem()] * 3,
         out_specs=vmem(),
-        compiler_params=params(),
+        compiler_params=params(16),
         cost_estimate=cost(2 * slots * foot_count * channels * 3, 0, 4 * slots * channels * 2),
         name="depart",
     )(slot, returned.reshape(slots, channels), observed)
@@ -436,19 +469,36 @@
     inside = jnp.stack([lat_at > 0, lat_at < lat_count - 1]).astype(f32)
     height, breadth = tile_rows + 2 * halo, tile_cols + 2 * halo
 
+    plain = pltpu.VMEM((height, breadth, levels), f32)
+    mixed = (height, breadth // 8, 8, levels)
+
+    def edges_body(*refs):
+        edges_kernel(halo, refs[:7], *refs[7:])
+
+    east, south = pl.pallas_call(
+        edges_body,
+        out_shape=(jax.ShapeDtypeStruct(mixed, f32),) * 2,
+        in_specs=[vmem()] * 7,
+        out_specs=(vmem(),) * 2,
+        scratch_shapes=[plain, pltpu.VMEM(mixed, f32)],
+        compiler_params=params(22),
+        cost_estimate=cost(4 * height * breadth * levels, 0, 12 * cells * levels),
+        name="edges",
+    )(diffusivity, *kappa_halos)
+
     def relax_body(inside_ref, *refs):
-        relax_kernel(halo, inside_ref, refs[:7], refs[7:14], *refs[14:])
+        relax_kernel(halo, inside_ref, refs[:7], *refs[7:])
 
     increment = pl.pallas_call(
         relax_body,
         out_shape=jax.ShapeDtypeStruct((tile_rows, tile_cols, levels), f32),
-        in_specs=[smem()] + [vmem()] * 14,
+        in_specs=[smem()] + [vmem()] * 9,
         out_specs=vmem(),
-        scratch_shapes=[pltpu.VMEM((height, breadth, levels), f32)] * 4,
-        compiler_params=params(),
+        scratch_shapes=[plain, pltpu.VMEM(mixed, f32), pltpu.VMEM(mixed, f32)],
+        compiler_params=params(26),
         cost_estimate=cost(10 * STEPS * height * breadth * levels, 0, 16 * cells * levels),
         name="relax",
-    )(inside, field, *field_halos, diffusivity, *kappa_halos)
+    )(inside, field, *field_halos, east, south)
     return (departure, increment)
 
 

time: 165 us -> 143 us (0.87)
  Pallas kernels: 98.6 us -> 71.2 us
  starting transfers between devices: 34.7 us -> 38.2 us
  local copies, waits for them, and re-layouts: 3.86 us -> 6.65 us
    pallas_call x1, Pallas kernels: 74.9 us -> 54 us  [local(): pl.pallas_call(functools.partial(column_kernel, capacity, halo), out_shap...]
    ppermute x2, waiting for transfers between devices: 7.56 us -> 0.35 us  [halos(): south = lax.ppermute(top, 'lat', lat_down)]
    ppermute x2, waiting for transfers between devices: 6.86 us -> 0.01 us  [halos(): lax.ppermute(jnp.concatenate([north[:, :halo], south[:, :halo]], axis=0),...]
    pallas_call x1, Pallas kernels: 17.3 us -> 10.7 us  [local(): pl.pallas_call(relax_body, out_shape=jax.ShapeDtypeStruct((tile_rows, til...]
    all_to_all x1, waiting for transfers between devices: 11.8 us -> 16.8 us  [local(): lax.all_to_all(send, ('lat', 'lon'), split_axis=0, concat_axis=0, tiled=T...]
    ppermute x2, waiting for transfers between devices: 0.01 us -> 4.88 us  [halos(): lax.ppermute(jnp.concatenate([north[:, -halo:], south[:, -halo:]], axis=0...]
    ppermute x2, starting transfers between devices: 4.64 us -> 9.17 us  [halos(): lax.ppermute(jnp.concatenate([north[:, :halo], south[:, :halo]], axis=0),...]
    ppermute x2, waiting for transfers between devices: 0.01 us -> 2.91 us  [halos(): north = lax.ppermute(bottom, 'lat', lat_up)]
  transfers between devices with their start and end apart: 14 -> 14, of which waited for: 5 -> 4; matrix products, arithmetic and copies ran while one was open for 1% -> 1% of each run, Pallas kernels for 56% -> 47%
where the time goes in v2:
time: 143 us; the launch traced here: 142 us
  Pallas kernels  71.2 us (50%)
  starting transfers between devices  38.2 us (27%)
  waiting for transfers between devices  25 us (17%)
  local copies, waits for them, and re-layouts  6.65 us (5%)
    pallas_call x1, Pallas kernels, local(): pl.pallas_call(functools.partial(column_kernel, capacity, halo), out_shap...  54 us
    all_to_all x1, waiting for transfers between devices, local(): lax.all_to_all(send, ('lat', 'lon'), split_axis=0, concat_axis=0, tiled=T...  16.8 us
    pallas_call x1, Pallas kernels, local(): pl.pallas_call(relax_body, out_shape=jax.ShapeDtypeStruct((tile_rows, til...  10.7 us
    ppermute x2, starting transfers between devices, halos(): lax.ppermute(jnp.concatenate([north[:, :halo], south[:, :halo]], axis=0),...  9.17 us
    all_to_all x1, starting transfers between devices, local(): lax.all_to_all(send, ('lat', 'lon'), split_axis=0, concat_axis=0, tiled=T...  7.08 us
    ppermute x2, starting transfers between devices, halos(): east = lax.ppermute(left, 'lon', lon_down)  6.85 us
    ppermute x2, starting transfers between devices, halos(): north = lax.ppermute(bottom, 'lat', lat_up)  6.54 us
    unnamed x18, local copies, waits for them, and re-layouts  4.95 us
  transfers between devices with their start and end apart: 14, of which 4 were waited for; matrix products, arithmetic and copies ran while one was open for 1% of the time, Pallas kernels for 47%

profile of v2, /device:TPU:1, one launch (start us, length us, event | category | flops | bytes accessed | tf_op | source)
XLA Modules:
  0.0 142.1 jit_solution(7328324939947335469)
XLA Ops:
  0.7 1.1 copy-done.2
  1.7 0.9 copy-done.3
  2.7 0.7 copy-done.5
  3.4 0.7 copy-done.6
  4.1 0.7 copy-done.7
  4.8 2.3 %pack.1 = (f32[32,40,128]{2,1,0:T(8,128)}, s32[1,512]{1,0:T(1,128)S(1)}) custom-call(s32[1]{0:T(128)} %bitcast.lane_ref, s32[1,512]{1,0:T(1,128)S(1)} %bitcast.11, s32[1,512]{1,0:T(1,128)S(1)} %bitcast.12, f32[4,512]{1,0:T(4,128)S(1)} %bitcast.10, f32[512,128]{1,0:T(8,128)S(1)} %copy-done.3, s32[512,128]{1,0:T(8,128)S(1)} %copy-done.2), custom_call_target="tpu_custom_call" | custom-call | flops 402653184 | bytes 1572864 | tf_op jit(solution)/shard_map/pack/pallas_call | solution.py:390
  7.1 7.1 %all-to-all-start = ((f32[32,40,128]{2,1,0:T(8,128)}), f32[32,40,128]{2,1,0:T(8,128)S(1)}, u32[]{:S(2)}, u32[]{:S(2)}) async-start(f32[32,40,128]{2,1,0:T(8,128)} %get-tuple-element.18), calls=%async_computation | async-start | bytes 1310720 | tf_op jit(solution)/shard_map/all_to_all | solution.py:406
  14.2 0.9 fusion.1
  15.0 0.8 fusion
  15.9 16.8 %all-to-all-done.recv_ref = f32[32,40,128]{2,1,0:T(8,128)S(1)} async-done(((f32[32,40,128]{2,1,0:T(8,128)}), f32[32,40,128]{2,1,0:T(8,128)S(1)}, u32[]{:S(2)}, u32[]{:S(2)}) %all-to-all-start) | async-done | bytes 655392 | tf_op jit(solution)/shard_map/all_to_all | solution.py:406
  32.7 0.8 copy-done.8
  33.5 2.8 %collective-permute-start.6 = (f32[8,64,128]{2,1,0:T(8,128)}, f32[8,64,128]{2,1,0:T(8,128)S(1)}, u32[]{:S(2)}, u32[]{:S(2)}) collective-permute-start(f32[8,64,128]{2,1,0:T(8,128)} %get-tuple-element.26), channel_id=1, source_target_pairs={{0,8},{8,16},{16,24},{1,9},{9,17},{17,25},{2,10},{10,18},{18,26},{... | collective-permute-start | bytes 786440 | tf_op jit(solution)/shard_map/ppermute | solution.py:360
  36.3 1.9 %collective-permute-start.7 = (f32[8,64,128]{2,1,0:T(8,128)}, f32[8,64,128]{2,1,0:T(8,128)S(1)}, u32[]{:S(2)}, u32[]{:S(2)}) collective-permute-start(f32[8,64,128]{2,1,0:T(8,128)} %get-tuple-element.27), channel_id=1, source_target_pairs={{8,0},{16,8},{24,16},{9,1},{17,9},{25,17},{10,2},{18,10},{26,18},{... | collective-permute-start | bytes 786440 | tf_op jit(solution)/shard_map/ppermute | solution.py:361
  38.3 0.7 collective-permute-start.8
  39.0 3.5 %collective-permute-start.9 = (f32[64,8,128]{2,1,0:T(8,128)}, f32[64,8,128]{2,1,0:T(8,128)}, u32[]{:S(2)}, u32[]{:S(2)}) collective-permute-start(f32[64,8,128]{2,1,0:T(8,128)} %get-tuple-element.29), channel_id=1, source_target_pairs={{1,0},{2,1},{3,2},{4,3},{5,4},{6,5},{7,6},{0,7},{9,8},{10,9},{11,1... | collective-permute-start | bytes 786440 | tf_op jit(solution)/shard_map/ppermute | solution.py:359
  42.5 54.0 %column.1 = (f32[32,32,128]{2,1,0:T(8,128)}, f32[64,64,128]{2,1,0:T(8,128)}, f32[8,64,128]{2,1,0:T(8,128)}, f32[8,64,128]{2,1,0:T(8,128)}, f32[64,8,128]{2,1,0:T(8,128)}, /*index=5*/f32[64,8,128]{2,1,0:T(8,128)}) custom-call(f32[32,40,128]{2,1,0:T(8,128)} %copy-done.8, bf16[64,64,128]{2,1,0:T(8,128)(2,1)} %background_ref.1, f32[128,128]{1,0:T(8,128)} %absorb_ref.1, ...), custom_call_target="tpu_custom_call" | custom-call | flops 234881024 | bytes 6291456 | tf_op jit(solution)/shard_map/column/pallas_call | solution.py:415
  96.5 2.7 %all-to-all-start.1 = ((f32[32,32,128]{2,1,0:T(8,128)}), f32[32,32,128]{2,1,0:T(8,128)S(1)}, u32[]{:S(2)}, u32[]{:S(2)}) async-start(f32[32,32,128]{2,1,0:T(8,128)} %get-tuple-element.20), calls=%async_computation.1 | async-start | bytes 1048576 | tf_op jit(solution)/shard_map/all_to_all | solution.py:455
  99.2 3.8 %collective-permute-start = (f32[8,64,128]{2,1,0:T(8,128)}, f32[8,64,128]{2,1,0:T(8,128)S(1)}, u32[]{:S(2)}, u32[]{:S(2)}) collective-permute-start(f32[8,64,128]{2,1,0:T(8,128)} %get-tuple-element.22), channel_id=1, source_target_pairs={{0,8},{8,16},{16,24},{1,9},{9,17},{17,25},{2,10},{10,18},{18,26},{... | collective-permute-start | bytes 786440 | tf_op jit(solution)/shard_map/ppermute | solution.py:360
  103.0 1.9 %collective-permute-start.1 = (f32[8,64,128]{2,1,0:T(8,128)}, f32[8,64,128]{2,1,0:T(8,128)S(1)}, u32[]{:S(2)}, u32[]{:S(2)}) collective-permute-start(f32[8,64,128]{2,1,0:T(8,128)} %get-tuple-element.23), channel_id=1, source_target_pairs={{8,0},{16,8},{24,16},{9,1},{17,9},{25,17},{10,2},{18,10},{26,18},{... | collective-permute-start | bytes 786440 | tf_op jit(solution)/shard_map/ppermute | solution.py:361
  104.9 1.0 collective-permute-start.2
  106.0 2.9 %collective-permute-done.refs_1_ = f32[8,64,128]{2,1,0:T(8,128)S(1)} collective-permute-done((f32[8,64,128]{2,1,0:T(8,128)}, f32[8,64,128]{2,1,0:T(8,128)S(1)}, u32[]{:S(2)}, u32[]{:S(2)}) %collective-permute-start) | collective-permute-done | bytes 262176 | tf_op jit(solution)/shard_map/ppermute | solution.py:360
  108.9 3.3 %collective-permute-start.3 = (f32[64,8,128]{2,1,0:T(8,128)}, f32[64,8,128]{2,1,0:T(8,128)S(1)}, u32[]{:S(2)}, u32[]{:S(2)}) collective-permute-start(f32[64,8,128]{2,1,0:T(8,128)} %get-tuple-element.25), channel_id=1, source_target_pairs={{1,0},{2,1},{3,2},{4,3},{5,4},{6,5},{7,6},{0,7},{9,8},{10,9},{11,1... | collective-permute-start | bytes 786440 | tf_op jit(solution)/shard_map/ppermute | solution.py:359
  112.2 0.3 collective-permute-done.1.refs_2_
  112.6 0.3 collective-permute-start.10
  112.9 3.9 %collective-permute-start.11 = (f32[16,8,128]{2,1,0:T(8,128)S(1)}, f32[16,8,128]{2,1,0:T(8,128)S(1)}, u32[]{:S(2)}, u32[]{:S(2)}) collective-permute-start(f32[16,8,128]{2,1,0:T(8,128)S(1)} %pad_maximum_fusion.3), channel_id=1, source_target_pairs={{1,0},{2,1},{3,2},{4,3},{5,4},{6,5},{7,6},{0,7},{9,8},{10,9},{11,1... | collective-permute-start | bytes 196616 | tf_op jit(solution)/shard_map/ppermute | solution.py:365
  116.8 4.9 %collective-permute-done.10.refs_5_ = f32[16,8,128]{2,1,0:T(8,128)S(1)} collective-permute-done((f32[16,8,128]{2,1,0:T(8,128)S(1)}, f32[16,8,128]{2,1,0:T(8,128)S(1)}, u32[]{:S(2)}, u32[]{:S(2)}) %collective-permute-start.10) | collective-permute-done | bytes 65568 | tf_op jit(solution)/shard_map/ppermute | solution.py:362
  121.7 5.2 %collective-permute-start.5 = (f32[16,8,128]{2,1,0:T(8,128)S(1)}, f32[16,8,128]{2,1,0:T(8,128)S(1)}, u32[]{:S(2)}, u32[]{:S(2)}) collective-permute-start(f32[16,8,128]{2,1,0:T(8,128)S(1)} %pad_maximum_fusion.1), channel_id=1, source_target_pairs={{1,0},{2,1},{3,2},{4,3},{5,4},{6,5},{7,6},{0,7},{9,8},{10,9},{11,1... | collective-permute-start | bytes 196616 | tf_op jit(solution)/shard_map/ppermute | solution.py:365
  126.9 0.1 add_convert_fusion.inside_ref
  127.0 2.5 %edges.1 = (f32[80,10,8,128]{3,2,1,0:T(8,128)S(1)}, f32[80,10,8,128]{3,2,1,0:T(8,128)S(1)}) custom-call(f32[64,64,128]{2,1,0:T(8,128)S(1)} %copy-done, f32[8,64,128]{2,1,0:T(8,128)S(1)} %collective-permute-done.6.refs_1_, f32[8,64,128]{2,1,0:T(8,128)S(1)} %collective-permute-done.7.refs_2_, f32[64,8,128]{2,1,0:T(8,128)S(1)} %collective-permute-done.8.refs_3_, ...), custom_call_target="tpu_custom_call" | custom-call | flops 3276800 | bytes 6291456 | tf_op jit(solution)/shard_map/edges/pallas_call | solution.py:478
  129.6 0.0 copy-start.4
  129.6 10.7 %relax.1 = f32[64,64,128]{2,1,0:T(8,128)} custom-call(f32[2]{0:T(128)S(1)} %add_convert_fusion.inside_ref, f32[64,64,128]{2,1,0:T(8,128)S(1)} %copy-done.1, f32[8,64,128]{2,1,0:T(8,128)S(1)} %collective-permute-done.refs_1_, f32[8,64,128]{2,1,0:T(8,128)S(1)} %collective-permute-done.1.refs_2_, f32[64,8,128]{2,1,0:T(8,128)S(1)} %collective-permute-done.2.refs_3_, ...), custom_call_target="tpu_custom_call" | custom-call | flops 65536000 | bytes 8388608 | tf_op jit(solution)/shard_map/relax/pallas_call | solution.py:492
  140.3 1.8 %depart.1 = f32[512,128]{1,0:T(8,128)} custom-call(s32[1,512]{1,0:T(1,128)S(1)} %get-tuple-element.17.slot_ref, f32[1024,128]{1,0:T(8,128)S(1)} %bitcast.9, f32[512,128]{1,0:T(8,128)S(1)} %copy-done.4), custom_call_target="tpu_custom_call" | custom-call | flops 402653184 | bytes 1048576 | tf_op jit(solution)/shard_map/depart/pallas_call | solution.py:458
  (30 shorter events, 0.1 us)
Async XLA Ops:
  0.6 13.5 %copy-start = (f32[64,64,128]{2,1,0:T(8,128)S(1)}, f32[64,64,128]{2,1,0:T(8,128)}, u32[]{:S(2)}) copy-start(f32[64,64,128]{2,1,0:T(8,128)} %refs_0_.1) | copy-start | bytes 6291460
  0.6 1.1 copy-start.2
  1.7 0.9 copy-start.3
  2.7 0.7 copy-start.5
  3.4 0.7 copy-start.6
  4.1 0.7 copy-start.7
  7.1 25.6 %all-to-all-start = ((f32[32,40,128]{2,1,0:T(8,128)}), f32[32,40,128]{2,1,0:T(8,128)S(1)}, u32[]{:S(2)}, u32[]{:S(2)}) async-start(f32[32,40,128]{2,1,0:T(8,128)} %get-tuple-element.18), calls=%async_computation | async-start | bytes 1310720 | tf_op jit(solution)/shard_map/all_to_all | solution.py:406
  32.7 0.8 copy-start.8
  33.5 69.4 %collective-permute-start.6 = (f32[8,64,128]{2,1,0:T(8,128)}, f32[8,64,128]{2,1,0:T(8,128)S(1)}, u32[]{:S(2)}, u32[]{:S(2)}) collective-permute-start(f32[8,64,128]{2,1,0:T(8,128)} %get-tuple-element.26), channel_id=1, source_target_pairs={{0,8},{8,16},{16,24},{1,9},{9,17},{17,25},{2,10},{10,18},{18,26},{... | collective-permute-start | bytes 786440 | tf_op jit(solution)/shard_map/ppermute | solution.py:360
  36.3 68.6 %collective-permute-start.7 = (f32[8,64,128]{2,1,0:T(8,128)}, f32[8,64,128]{2,1,0:T(8,128)S(1)}, u32[]{:S(2)}, u32[]{:S(2)}) collective-permute-start(f32[8,64,128]{2,1,0:T(8,128)} %get-tuple-element.27), channel_id=1, source_target_pairs={{8,0},{16,8},{24,16},{9,1},{17,9},{25,17},{10,2},{18,10},{26,18},{... | collective-permute-start | bytes 786440 | tf_op jit(solution)/shard_map/ppermute | solution.py:361
  38.3 74.6 %collective-permute-start.8 = (f32[64,8,128]{2,1,0:T(8,128)}, f32[64,8,128]{2,1,0:T(8,128)S(1)}, u32[]{:S(2)}, u32[]{:S(2)}) collective-permute-start(f32[64,8,128]{2,1,0:T(8,128)} %get-tuple-element.28), channel_id=1, source_target_pairs={{0,1},{1,2},{2,3},{3,4},{4,5},{5,6},{6,7},{7,0},{8,9},{9,10},{10,1... | collective-permute-start | bytes 786440 | tf_op jit(solution)/shard_map/ppermute | solution.py:358
  39.0 77.9 %collective-permute-start.9 = (f32[64,8,128]{2,1,0:T(8,128)}, f32[64,8,128]{2,1,0:T(8,128)}, u32[]{:S(2)}, u32[]{:S(2)}) collective-permute-start(f32[64,8,128]{2,1,0:T(8,128)} %get-tuple-element.29), channel_id=1, source_target_pairs={{1,0},{2,1},{3,2},{4,3},{5,4},{6,5},{7,6},{0,7},{9,8},{10,9},{11,1... | collective-permute-start | bytes 786440 | tf_op jit(solution)/shard_map/ppermute | solution.py:359
  96.5 43.8 %all-to-all-start.1 = ((f32[32,32,128]{2,1,0:T(8,128)}), f32[32,32,128]{2,1,0:T(8,128)S(1)}, u32[]{:S(2)}, u32[]{:S(2)}) async-start(f32[32,32,128]{2,1,0:T(8,128)} %get-tuple-element.20), calls=%async_computation.1 | async-start | bytes 1048576 | tf_op jit(solution)/shard_map/all_to_all | solution.py:455
  99.2 9.7 %collective-permute-start = (f32[8,64,128]{2,1,0:T(8,128)}, f32[8,64,128]{2,1,0:T(8,128)S(1)}, u32[]{:S(2)}, u32[]{:S(2)}) collective-permute-start(f32[8,64,128]{2,1,0:T(8,128)} %get-tuple-element.22), channel_id=1, source_target_pairs={{0,8},{8,16},{16,24},{1,9},{9,17},{17,25},{2,10},{10,18},{18,26},{... | collective-permute-start | bytes 786440 | tf_op jit(solution)/shard_map/ppermute | solution.py:360
  103.0 9.6 %collective-permute-start.1 = (f32[8,64,128]{2,1,0:T(8,128)}, f32[8,64,128]{2,1,0:T(8,128)S(1)}, u32[]{:S(2)}, u32[]{:S(2)}) collective-permute-start(f32[8,64,128]{2,1,0:T(8,128)} %get-tuple-element.23), channel_id=1, source_target_pairs={{8,0},{16,8},{24,16},{9,1},{17,9},{25,17},{10,2},{18,10},{26,18},{... | collective-permute-start | bytes 786440 | tf_op jit(solution)/shard_map/ppermute | solution.py:361
  104.9 24.7 %copy-start.1 = (f32[64,64,128]{2,1,0:T(8,128)S(1)}, f32[64,64,128]{2,1,0:T(8,128)}, u32[]{:S(2)}) copy-start(f32[64,64,128]{2,1,0:T(8,128)} %get-tuple-element.21.refs_0_) | copy-start | bytes 6291460
  104.9 24.6 %collective-permute-start.2 = (f32[64,8,128]{2,1,0:T(8,128)}, f32[64,8,128]{2,1,0:T(8,128)S(1)}, u32[]{:S(2)}, u32[]{:S(2)}) collective-permute-start(f32[64,8,128]{2,1,0:T(8,128)} %get-tuple-element.24), channel_id=1, source_target_pairs={{0,1},{1,2},{2,3},{3,4},{4,5},{5,6},{6,7},{7,0},{8,9},{9,10},{10,1... | collective-permute-start | bytes 786440 | tf_op jit(solution)/shard_map/ppermute | solution.py:358
  108.9 20.7 %collective-permute-start.3 = (f32[64,8,128]{2,1,0:T(8,128)}, f32[64,8,128]{2,1,0:T(8,128)S(1)}, u32[]{:S(2)}, u32[]{:S(2)}) collective-permute-start(f32[64,8,128]{2,1,0:T(8,128)} %get-tuple-element.25), channel_id=1, source_target_pairs={{1,0},{2,1},{3,2},{4,3},{5,4},{6,5},{7,6},{0,7},{9,8},{10,9},{11,1... | collective-permute-start | bytes 786440 | tf_op jit(solution)/shard_map/ppermute | solution.py:359
  112.6 9.2 %collective-permute-start.10 = (f32[16,8,128]{2,1,0:T(8,128)S(1)}, f32[16,8,128]{2,1,0:T(8,128)S(1)}, u32[]{:S(2)}, u32[]{:S(2)}) collective-permute-start(f32[16,8,128]{2,1,0:T(8,128)S(1)} %pad_maximum_fusion.2), channel_id=1, source_target_pairs={{0,1},{1,2},{2,3},{3,4},{4,5},{5,6},{6,7},{7,0},{8,9},{9,10},{10,1... | collective-permute-start | bytes 196616 | tf_op jit(solution)/shard_map/ppermute | solution.py:362
  112.9 14.1 %collective-permute-start.11 = (f32[16,8,128]{2,1,0:T(8,128)S(1)}, f32[16,8,128]{2,1,0:T(8,128)S(1)}, u32[]{:S(2)}, u32[]{:S(2)}) collective-permute-start(f32[16,8,128]{2,1,0:T(8,128)S(1)} %pad_maximum_fusion.3), channel_id=1, source_target_pairs={{1,0},{2,1},{3,2},{4,3},{5,4},{6,5},{7,6},{0,7},{9,8},{10,9},{11,1... | collective-permute-start | bytes 196616 | tf_op jit(solution)/shard_map/ppermute | solution.py:365
  116.8 12.7 %collective-permute-start.4 = (f32[16,8,128]{2,1,0:T(8,128)S(1)}, f32[16,8,128]{2,1,0:T(8,128)S(1)}, u32[]{:S(2)}, u32[]{:S(2)}) collective-permute-start(f32[16,8,128]{2,1,0:T(8,128)S(1)} %pad_maximum_fusion), channel_id=1, source_target_pairs={{0,1},{1,2},{2,3},{3,4},{4,5},{5,6},{6,7},{7,0},{8,9},{9,10},{10,1... | collective-permute-start | bytes 196616 | tf_op jit(solution)/shard_map/ppermute | solution.py:362
  121.7 7.9 %collective-permute-start.5 = (f32[16,8,128]{2,1,0:T(8,128)S(1)}, f32[16,8,128]{2,1,0:T(8,128)S(1)}, u32[]{:S(2)}, u32[]{:S(2)}) collective-permute-start(f32[16,8,128]{2,1,0:T(8,128)S(1)} %pad_maximum_fusion.1), channel_id=1, source_target_pairs={{1,0},{2,1},{3,2},{4,3},{5,4},{6,5},{7,6},{0,7},{9,8},{10,9},{11,1... | collective-permute-start | bytes 196616 | tf_op jit(solution)/shard_map/ppermute | solution.py:365
  129.6 10.7 %copy-start.4 = (f32[512,128]{1,0:T(8,128)S(1)}, f32[512,128]{1,0:T(8,128)}, u32[]{:S(2)}) copy-start(f32[512,128]{1,0:T(8,128)} %observed_ref.3) | copy-start | bytes 786436
